TPU v7x, 256 devices: a whole 4x4x8 slice. The times are simulated.
256 devices in a mesh: dp: 4 (over x), expert: 64 (over y, z, core).
Axes of the slice: x: 4, y: 4, z: 8, core: 2. Of those that a mesh axis runs over, the one named last changes fastest.
Arguments:
- tokens: bfloat16 [8192, 4096], P('expert', 'dp'), may hold values from -6 to 6
- routes: int32 [8192, 4], P('expert'), may hold values from 0 to 63, all different within a row; in each aligned block of 128 rows (0 to 127, 128 to 255, ...) at most 16 rows name the same one
- route_weights: float32 [8192, 4], P('expert'), may hold values from 0.1 to 1
- gate_weight: bfloat16 [64, 4096, 1536], P('expert', None, 'dp'), may hold values from -0.09375 to 0.09375
- up_weight: bfloat16 [64, 4096, 1536], P('expert', None, 'dp'), may hold values from -0.09375 to 0.09375
- down_weight: bfloat16 [64, 1536, 4096], P('expert', 'dp'), may hold values from -0.15625 to 0.15625
- sketch_basis: bfloat16 [1536, 128], P('dp'), may hold values from -0.15625 to 0.15625
Outputs:
- mixed: bfloat16 [8192, 4096], P('expert', 'dp')
- sketch: float32 [64, 128, 1536], P('expert', None, 'dp')
Inputs may be any that keep to these rules, and one draw needn't show every extreme that they name: `routes`: each row names 4 different experts; within the rows of one device no expert is named more than 16 times, a bound that some block reaches.
All inputs are finite; a program needn't handle non-finite values.
Results may differ from a plain program's by a relative error of at most 0.017.
Values may be sent and summed in bfloat16 or wider, within the bound.
No kernel may reach another device: no remote copies, remote signals or barrier semaphores. Data moves between devices by JAX's collectives and lax.ppermute only.
A program may use at most 128 MiB of HBM per device.

v0:
```python
import jax
import jax.numpy as jnp
from jax import lax
from jax.sharding import PartitionSpec as P

ridge_term = 1.0


def gram_matrix(factor_rows):
    return jnp.dot(factor_rows.T, factor_rows, precision=lax.Precision.HIGHEST)


def body(tokens, routes, route_weights, gate_weight, up_weight, down_weight, sketch_basis):
    owners = lax.axis_size("expert")
    token_count, route_count = routes.shape
    pair_count = token_count * route_count
    capacity = 2 * pair_count // owners
    slot_total = owners * capacity
    route_list = routes.reshape(-1)
    onehot = (route_list[:, None] == jnp.arange(owners, dtype=jnp.int32)[None, :]).astype(jnp.int32)
    before = jnp.cumsum(onehot, axis=0) - onehot
    slot_of = jnp.sum(before * onehot, axis=1)
    counts = jnp.sum(onehot, axis=0)
    target = route_list * capacity + slot_of
    source_pair = (
        jnp.zeros((slot_total,), jnp.int32).at[target].set(jnp.arange(pair_count, dtype=jnp.int32))
    )
    source_token = source_pair // route_count
    count_wire = counts.astype(jnp.bfloat16)
    features = lax.all_gather(tokens, "dp", axis=1, tiled=True)
    outgoing = features[source_token].reshape(owners, capacity, features.shape[1])
    arrived, arrived_counts = (
        lax.all_to_all(outgoing, "expert", split_axis=0, concat_axis=0, tiled=True),
        lax.all_to_all(count_wire, "expert", split_axis=0, concat_axis=0, tiled=True),
    )
    width = arrived.shape[2]
    live_count = arrived_counts.astype(jnp.int32)
    live_mask = (jnp.arange(capacity, dtype=jnp.int32)[None, :] < live_count[:, None]).reshape(-1)
    slot_rows = jnp.where(
        live_mask[:, None], arrived.reshape(slot_total, width), jnp.zeros((), jnp.bfloat16)
    )
    gate_local = gate_weight[0]
    up_local = up_weight[0]
    down_local = down_weight[0]
    gate_val = jnp.dot(slot_rows, gate_local, preferred_element_type=jnp.float32)
    up_val = jnp.dot(slot_rows, up_local, preferred_element_type=jnp.float32)
    hidden_block = (jax.nn.silu(gate_val) * up_val).astype(jnp.bfloat16)
    partial_value = jnp.dot(hidden_block, down_local, preferred_element_type=jnp.float32)
    sums = lax.psum_scatter(
        partial_value.reshape(owners, capacity, width).astype(jnp.bfloat16),
        "dp",
        scatter_dimension=2,
        tiled=True,
    )
    returned = lax.all_to_all(sums, "expert", split_axis=0, concat_axis=0, tiled=True)
    picked = returned.reshape(slot_total, returned.shape[2])[target]
    weighted = jnp.einsum(
        "tkd,tk->td",
        picked.reshape(token_count, route_count, returned.shape[2]).astype(jnp.float32),
        route_weights,
    )
    mixed = weighted.astype(jnp.bfloat16)
    sketch_part = jnp.dot(hidden_block, sketch_basis, preferred_element_type=jnp.float32)
    sketch_width = sketch_part.shape[1]
    eye_matrix = jnp.eye(sketch_width, dtype=jnp.float32)
    sketch_full = lax.psum(sketch_part.astype(jnp.bfloat16), "dp").astype(jnp.float32)
    lower_factor = jnp.linalg.cholesky(gram_matrix(sketch_full) + ridge_term * eye_matrix)
    projected = jnp.dot(
        sketch_full.T, hidden_block.astype(jnp.float32), precision=lax.Precision.HIGHEST
    )
    whitened = jax.scipy.linalg.solve_triangular(lower_factor, projected, lower=True)
    return (mixed, whitened[None])


def solution(mesh):
    return jax.shard_map(
        body,
        mesh=mesh,
        in_specs=(
            P("expert", "dp"),
            P("expert", None),
            P("expert", None),
            P("expert", None, "dp"),
            P("expert", None, "dp"),
            P("expert", "dp", None),
            P("dp", None),
        ),
        out_specs=(P("expert", "dp"), P("expert", None, "dp")),
        check_vma=False,
    )
```

profile of v0, /device:TPU:1, one launch (start us, length us, event | category | flops | bytes accessed | tf_op | source)
XLA Modules:
  0.0 462.6 jit_solution(337429624355263726)
XLA Ops:
  7.2 0.0 copy-start
  7.2 0.0 all-gather.2.cloned.1.call-start
  7.2 0.7 all-gather.2.cloned.1.call-update
  7.9 1.0 copy.21
  8.9 0.1 eq.33
  9.0 0.1 eq.29
  9.1 1.2 reduce-window.6
  10.3 0.2 slice_reduce_fusion
  10.6 0.2 convert_reduce_fusion
  10.8 0.7 copy.22
  11.5 13.2 %all-to-all-start = ((bf16[64,1,1]{2,1,0:T(2,128)(2,1)}), bf16[64,1,1]{2,1,0:T(2,128)(2,1)S(1)}, u32[]{:S(2)}, u32[]{:S(2)}) async-start(bf16[64,1,1]{2,1,0:T(2,128)(2,1)} %copy.22), calls=%async_computation | async-start | bytes 65536 | tf_op jit(solution)/shard_map/all_to_all | solution.py:34
  24.7 0.7 broadcast_multiply_fusion
  25.4 0.1 copy.23
  25.5 0.1 mul.28
  25.6 2.4 scatter_custom_fusion
  28.1 11.1 %all-gather.2.cloned.1.call-done = bf16[128,4096]{1,0:T(8,128)(2,1)} async-done(((bf16[128,1024]{1,0:T(8,128)(2,1)}), bf16[128,4096]{1,0:T(8,128)(2,1)}) %all-gather.2.cloned.1.call-update) | async-done | bytes 1048592 | tf_op jit(solution)/shard_map/all_gather | solution.py:30
  39.2 16.4 %gather_fusion = bf16[1024,4096]{1,0:T(8,128)(2,1)} fusion(bf16[128,4096]{1,0:T(8,128)(2,1)} %all-gather.2.cloned.1.call-done, s32[1024]{0:T(1024)S(1)} %fusion.15), kind=kCustom, calls=%fused_computation | custom fusion | bytes 16781312 | tf_op jit(solution)/shard_map/gather | solution.py:31
  55.7 11.8 %all-to-all-start.1 = ((bf16[64,16,4096]{2,1,0:T(8,128)(2,1)}), bf16[64,16,4096]{2,1,0:T(8,128)(2,1)}, u32[]{:S(2)}, u32[]{:S(2)}) async-start(bf16[64,16,4096]{2,1,0:T(8,128)(2,1)} %bitcast.60), calls=%async_computation.1 | async-start | bytes 16777216 | tf_op jit(solution)/shard_map/all_to_all | solution.py:33
  67.5 0.2 reduce-scatter.2.cloned.1.call-start
  67.7 1.2 convert_reduce_fusion.1
  68.9 0.1 iota_compare_fusion.5
  69.0 184.2 %all-to-all-done.1 = bf16[64,16,4096]{2,1,0:T(8,128)(2,1)} async-done(((bf16[64,16,4096]{2,1,0:T(8,128)(2,1)}), bf16[64,16,4096]{2,1,0:T(8,128)(2,1)}, u32[]{:S(2)}, u32[]{:S(2)}) %all-to-all-start.1) | async-done | bytes 8388640 | tf_op jit(solution)/shard_map/all_to_all | solution.py:33
  253.3 7.2 %broadcast_select_fusion = bf16[64,16,4096]{2,1,0:T(8,128)(2,1)} fusion(bf16[64,16,4096]{2,1,0:T(8,128)(2,1)} %all-to-all-done.1, pred[64,16]{1,0:T(8,128)(4,1)S(1)} %iota_compare_fusion.5), kind=kLoop, calls=%fused_computation.3 | loop fusion | flops 4194304 | bytes 16778240 | tf_op jit(solution)/shard_map/jit(_where)/select_n | solution.py:39
  260.5 8.0 %fusion.3 = f32[1024,384]{1,0:T(8,128)S(1)} fusion(bf16[1024,4096]{1,0:T(8,128)(2,1)} %bitcast.61, bf16[1,4096,384]{2,1,0:T(8,128)(2,1)} %param.10), kind=kOutput, calls=%fused_computation.8 | convolution fusion | flops 3221225472 | bytes 13107200 | tf_op jit(solution)/shard_map/dot_general | solution.py:45
  268.5 4.6 multiply_convert_fusion
  273.1 0.9 copy-done.2
  273.9 6.6 %convolution_convert_fusion = bf16[64,16,4096]{2,1,0:T(8,128)(2,1)} fusion(bf16[64,16,384]{2,1,0:T(8,128)(2,1)S(1)} %bitcast.63, bf16[1,384,4096]{2,1,0:T(8,128)(2,1)S(1)} %copy-done), kind=kOutput, calls=%fused_computation.4 | convolution fusion | flops 3225419776 | bytes 12320768 | tf_op jit(solution)/shard_map/dot_general | solution.py:48
  280.6 0.0 reduce-scatter.2.cloned.1.call-update
  280.6 0.0 copy-start.4
  280.6 78.8 %reduce-scatter.2.cloned.1.call-done = bf16[64,16,1024]{2,1,0:T(8,128)(2,1)} async-done(((bf16[64,16,4096]{2,1,0:T(8,128)(2,1)}), bf16[64,16,1024]{2,1,0:T(8,128)(2,1)}) %reduce-scatter.2.cloned.1.call-update) | async-done | bytes 2097168 | tf_op jit(solution)/shard_map/reduce_scatter | solution.py:49
  359.4 10.8 %all-to-all-start.2 = ((bf16[64,16,1024]{2,1,0:T(8,128)(2,1)}), bf16[64,16,1024]{2,1,0:T(8,128)(2,1)}, u32[]{:S(2)}, u32[]{:S(2)}) async-start(bf16[64,16,1024]{2,1,0:T(8,128)(2,1)} %reduce-scatter.2.cloned.1.call-done), calls=%async_computation.3 | async-start | bytes 4194304 | tf_op jit(solution)/shard_map/all_to_all | solution.py:55
  370.3 0.3 all-reduce.2.cloned.1.call-start
  370.5 2.2 convolution_convert_fusion.1
  372.8 0.0 all-reduce.2.cloned.1.call-update
  372.8 0.2 copy.27
  373.0 45.9 %all-reduce.2.cloned.1.call-done = bf16[1024,128]{1,0:T(8,128)(2,1)} async-done(((bf16[1024,128]{1,0:T(8,128)(2,1)}), bf16[1024,128]{1,0:T(8,128)(2,1)}) %all-reduce.2.cloned.1.call-update) | async-done | bytes 262160 | tf_op jit(solution)/shard_map/psum | solution.py:66
  418.9 1.3 fusion.20
  420.2 0.1 copy.26
  420.3 11.7 %cholesky.17 = f32[128,128]{1,0:T(8,128)S(1)} custom-call(f32[128,128]{1,0:T(8,128)S(1)} %fusion.13), custom_call_target="Cholesky" | custom-call | tf_op jit(solution)/shard_map/jit(cholesky)/cholesky | solution.py:67
  432.1 0.6 compare_reduce_fusion
  432.7 0.7 fusion.10
  433.4 9.8 %custom-call.7 = f32[1,128,128]{1,2,0:T(8,128)S(1)} custom-call(f32[1,128,128]{2,1,0:T(8,128)S(1)} %fusion.10), custom_call_target="InvertDiagBlocksLowerTriangular" | custom-call | tf_op jit(solution)/shard_map/jit(_solve_triangular)/triangular_solve | solution.py:71
  443.2 1.5 fusion.21
  444.7 1.0 convolution_bitcast_fusion
  445.8 5.3 %gather_fusion.1 = bf16[512,1024]{1,0:T(8,128)(2,1)} fusion(bf16[1024,1024]{1,0:T(8,128)(2,1)} %bitcast.11, s32[1024]{0:T(1024)S(1)} %pad_clamp_fusion), kind=kCustom, calls=%fused_computation.1 | custom fusion | bytes 2099200 | tf_op jit(solution)/shard_map/gather | solution.py:56
  451.1 2.3 reshape.115
  453.4 1.9 fusion.19
  455.3 0.8 copy.32
  (21 shorter events, 0.2 us)
Async XLA Ops:
  7.2 266.8 %copy-start = (bf16[1,384,4096]{2,1,0:T(8,128)(2,1)S(1)}, bf16[1,384,4096]{2,1,0:T(8,128)(2,1)}, u32[]{:S(2)}) copy-start(bf16[1,384,4096]{2,1,0:T(8,128)(2,1)} %param.12) | copy-start | bytes 9437188
  7.2 32.1 %all-gather.2.cloned.1.call-start = ((), (), s32[]{:S(2)}) async-start(), calls=%async_computation.4 | async-start | bytes 1310720 | tf_op jit(solution)/shard_map/all_gather | solution.py:30
  11.5 44.2 %all-to-all-start = ((bf16[64,1,1]{2,1,0:T(2,128)(2,1)}), bf16[64,1,1]{2,1,0:T(2,128)(2,1)S(1)}, u32[]{:S(2)}, u32[]{:S(2)}) async-start(bf16[64,1,1]{2,1,0:T(2,128)(2,1)} %copy.22), calls=%async_computation | async-start | bytes 65536 | tf_op jit(solution)/shard_map/all_to_all | solution.py:34
  55.7 197.6 %all-to-all-start.1 = ((bf16[64,16,4096]{2,1,0:T(8,128)(2,1)}), bf16[64,16,4096]{2,1,0:T(8,128)(2,1)}, u32[]{:S(2)}, u32[]{:S(2)}) async-start(bf16[64,16,4096]{2,1,0:T(8,128)(2,1)} %bitcast.60), calls=%async_computation.1 | async-start | bytes 16777216 | tf_op jit(solution)/shard_map/all_to_all | solution.py:33
  67.5 291.9 %reduce-scatter.2.cloned.1.call-start = ((), (), s32[]{:S(2)}) async-start(), calls=%async_computation.5 | async-start | bytes 10485760 | tf_op jit(solution)/shard_map/reduce_scatter | solution.py:49
  260.5 8.0 %copy-start.1 = (bf16[64,16,4096]{2,1,0:T(8,128)(2,1)S(1)}, bf16[64,16,4096]{2,1,0:T(8,128)(2,1)}, u32[]{:S(2)}) copy-start(bf16[64,16,4096]{2,1,0:T(8,128)(2,1)} %broadcast_select_fusion) | copy-start | bytes 25165828
  260.5 8.0 %copy-start.5 = (bf16[1,4096,384]{2,1,0:T(8,128)(2,1)S(1)}, bf16[1,4096,384]{2,1,0:T(8,128)(2,1)}, u32[]{:S(2)}) copy-start(bf16[1,4096,384]{2,1,0:T(8,128)(2,1)} %param.11) | copy-start | bytes 9437188
  273.1 0.9 copy-start.2
  280.6 89.9 %copy-start.3 = (bf16[384,128]{1,0:T(8,128)(2,1)S(1)}, bf16[384,128]{1,0:T(8,128)(2,1)}, u32[]{:S(2)}) copy-start(bf16[384,128]{1,0:T(8,128)(2,1)} %param.13) | copy-start | bytes 294916
  280.6 92.2 %copy-start.4 = (f32[128,4]{0,1:T(4,128)S(1)}, f32[128,4]{0,1:T(4,128)}, u32[]{:S(2)}) copy-start(f32[128,4]{0,1:T(4,128)} %param.9) | copy-start | bytes 6148
  359.4 86.4 %all-to-all-start.2 = ((bf16[64,16,1024]{2,1,0:T(8,128)(2,1)}), bf16[64,16,1024]{2,1,0:T(8,128)(2,1)}, u32[]{:S(2)}, u32[]{:S(2)}) async-start(bf16[64,16,1024]{2,1,0:T(8,128)(2,1)} %reduce-scatter.2.cloned.1.call-done), calls=%async_computation.3 | async-start | bytes 4194304 | tf_op jit(solution)/shard_map/all_to_all | solution.py:55
  370.3 48.6 %all-reduce.2.cloned.1.call-start = ((), (), s32[]{:S(2)}) async-start(), calls=%async_computation.6 | async-start | bytes 524288 | tf_op jit(solution)/shard_map/psum | solution.py:66
Sparse Core Ops, SparseCore 0:
  9.8 29.3 all-gather.1
  280.7 78.6 reduce-scatter.1
  374.0 44.8 all-reduce.1
where the time goes:
time: 464 us; the launch traced here: 463 us
  waiting for transfers between devices  321 us (69%)
  starting transfers between devices  36.3 us (8%)
  other arithmetic  33.6 us (7%)
  local copies, waits for them, and re-layouts  30.8 us (7%)
  matrix products  27.2 us (6%)
  between operations  14 us (3%)
    all_to_all x1, waiting for transfers between devices, body(): lax.all_to_all(outgoing, 'expert', split_axis=0, concat_axis=0, tiled=True)  184 us
    reduce_scatter x1, waiting for transfers between devices, body(): lax.psum_scatter(partial_value.reshape(owners, capacity, width).astype(jn...  78.8 us
    psum x1, waiting for transfers between devices, body(): lax.psum(sketch_part.astype(jnp.bfloat16), 'dp').astype(jnp.float32)  45.9 us
    gather x1, local copies, waits for them, and re-layouts, body(): features[source_token].reshape(owners, capacity, features.shape[1])  16.4 us
    all_to_all x1, starting transfers between devices, body(): lax.all_to_all(count_wire, 'expert', split_axis=0, concat_axis=0, tiled=T...  13.2 us
    another operation x3, other arithmetic, body(): jnp.linalg.cholesky(gram_matrix(sketch_full) + ridge_term * eye_matrix)  12.4 us
    all_to_all x1, starting transfers between devices, body(): lax.all_to_all(outgoing, 'expert', split_axis=0, concat_axis=0, tiled=True)  11.8 us
    all_gather x1, waiting for transfers between devices, body(): features = lax.all_gather(tokens, 'dp', axis=1, tiled=True)  11.1 us
  transfers between devices with their start and end apart: 6, of which 4 were waited for; matrix products, arithmetic and copies ran while one was open for 12% of the time, Pallas kernels for 0%

commit v1 on v0

v1 whole, which is shorter than its diff:
```python
import functools

import jax
import jax.numpy as jnp
from jax import lax
from jax.experimental import pallas as pl
from jax.experimental.pallas import tpu as pltpu
from jax.sharding import PartitionSpec as P

ridge_term = 1.0
SLOT_CHUNKS = 1
VMEM = pl.BlockSpec(memory_space=pltpu.VMEM)


def slot_codes(routes, experts):
    tokens, top = routes.shape
    expert_of = lax.broadcasted_iota(jnp.int32, (tokens, experts), 1)
    hits = [(routes[:, k : k + 1] == expert_of).astype(jnp.float32) for k in range(top)]
    hit = functools.reduce(jnp.add, hits)
    row = lax.broadcasted_iota(jnp.int32, (tokens, tokens), 0)
    column = lax.broadcasted_iota(jnp.int32, (tokens, tokens), 1)
    earlier = (row > column).astype(jnp.bfloat16)
    before = jnp.dot(earlier, hit.astype(jnp.bfloat16), preferred_element_type=jnp.float32)
    return hits, jnp.where(hit > 0.0, before, -1.0)


def spread(values, experts, slots):
    expert = lax.broadcasted_iota(jnp.int32, (experts, experts * slots), 0)
    first = expert * slots
    at = lax.broadcasted_iota(jnp.int32, (experts, experts * slots), 1)
    ones = jnp.where((at >= first) & (at < first + slots), 1.0, 0.0).astype(jnp.bfloat16)
    return jnp.dot(values.astype(jnp.bfloat16), ones, preferred_element_type=jnp.float32)


def slot_numbers(tokens, experts, slots, start):
    at = lax.broadcasted_iota(jnp.int32, (tokens, experts * slots), 1)
    return (lax.rem(at, slots) + start).astype(jnp.float32)


def dispatch_kernel(experts, slots, routes_ref, tokens_ref, *out_refs):
    _, code = slot_codes(routes_ref[...], experts)
    tokens = tokens_ref[...]
    wide = spread(code, experts, slots)
    for chunk, out_ref in enumerate(out_refs):
        numbers = slot_numbers(tokens.shape[0], experts, slots, chunk * slots)
        chosen = jnp.where(wide == numbers, 1.0, 0.0).T.astype(jnp.bfloat16)
        out_ref[...] = jnp.dot(chosen, tokens, preferred_element_type=jnp.float32).astype(out_ref.dtype)


def dispatch(routes, tokens, experts, slots, chunks):
    rows, width = experts * slots, tokens.shape[1]
    return pl.pallas_call(
        functools.partial(dispatch_kernel, experts, slots),
        out_shape=[jax.ShapeDtypeStruct((rows, width), tokens.dtype)] * chunks,
        in_specs=[VMEM] * 2,
        out_specs=[VMEM] * chunks,
        name="dispatch",
    )(routes, tokens)


def combine_kernel(experts, slots, routes_ref, weights_ref, *refs):
    out_ref = refs[-1]
    hits, code = slot_codes(routes_ref[...], experts)
    weights = weights_ref[...]
    weight = functools.reduce(jnp.add, [h * weights[:, k : k + 1] for k, h in enumerate(hits)])
    high = weight.astype(jnp.bfloat16)
    low = (weight - high.astype(jnp.float32)).astype(jnp.bfloat16)
    wide = spread(code, experts, slots)
    high_wide = spread(high, experts, slots)
    low_wide = spread(low, experts, slots)
    total = None
    for chunk, row_ref in enumerate(refs[:-1]):
        numbers = slot_numbers(weight.shape[0], experts, slots, chunk * slots)
        chosen = wide == numbers
        rows = row_ref[...]
        for part in (high_wide, low_wide):
            matrix = jnp.where(chosen, part, 0.0).astype(jnp.bfloat16)
            term = jnp.dot(matrix, rows, preferred_element_type=jnp.float32)
            total = term if total is None else total + term
    out_ref[...] = total.astype(out_ref.dtype)


def combine(routes, weights, rows, experts, slots):
    return pl.pallas_call(
        functools.partial(combine_kernel, experts, slots),
        out_shape=jax.ShapeDtypeStruct((routes.shape[0], rows[0].shape[1]), jnp.bfloat16),
        in_specs=[VMEM] * (2 + len(rows)),
        out_specs=VMEM,
        name="combine",
    )(routes, weights, *rows)


def hidden_kernel(rows_ref, gate_ref, up_ref, *refs):
    hidden_ref = refs[-1]
    parts, block, width = rows_ref.shape
    gate = up = None
    for part in range(parts):
        rows = rows_ref[part]
        cut = pl.ds(part * width, width)
        gate_term = jnp.dot(rows, gate_ref[cut, :], preferred_element_type=jnp.float32)
        up_term = jnp.dot(rows, up_ref[cut, :], preferred_element_type=jnp.float32)
        gate = gate_term if gate is None else gate + gate_term
        up = up_term if up is None else up + up_term
    at = pl.multiple_of(pl.program_id(0) * block, block)
    hidden_ref[pl.ds(at, block), :] = (gate / (1.0 + jnp.exp(-gate)) * up).astype(hidden_ref.dtype)
    for extra_ref in refs[:-1]:
        count = hidden_ref.shape[0] - extra_ref.shape[0]

        @pl.when(pl.program_id(0) == 0)
        def _():
            hidden_ref[count:, :] = extra_ref[...]


def hidden_of(rows, gate_weight, up_weight, extra):
    parts, count, width = rows.shape
    units = gate_weight.shape[1]
    block = min(256, count)
    whole = pl.BlockSpec(gate_weight.shape, lambda i: (0, 0))
    total = count + sum(e.shape[0] for e in extra)
    return pl.pallas_call(
        hidden_kernel,
        grid=(count // block,),
        out_shape=jax.ShapeDtypeStruct((total, units), jnp.bfloat16),
        in_specs=[pl.BlockSpec((parts, block, width), lambda i: (0, i, 0)), whole, whole]
        + [pl.BlockSpec(e.shape, lambda i: (0, 0)) for e in extra],
        out_specs=pl.BlockSpec((total, units), lambda i: (0, 0)),
        cost_estimate=pl.CostEstimate(
            flops=4 * parts * count * width * units,
            bytes_accessed=2 * parts * width * (count + 2 * units) + 2 * count * units,
            transcendentals=count * units,
        ),
        compiler_params=pltpu.CompilerParams(vmem_limit_bytes=48 << 20),
        name="hidden",
    )(rows, gate_weight, up_weight, *extra)


def output_kernel(me_ref, hidden_ref, *refs):
    out_ref = refs[-1]
    parts = hidden_ref.shape[0]
    total = None
    for shift, down_ref in enumerate(refs[:-1]):
        part = lax.rem(me_ref[0] + parts - shift, parts)
        term = jnp.dot(hidden_ref[part], down_ref[...], preferred_element_type=jnp.float32)
        total = term if total is None else total + term
    out_ref[...] = total.astype(out_ref.dtype)


def output_of(hidden, down, count):
    parts, _, units = hidden.shape
    width = down[0].shape[1]
    block = min(256, count)
    me = lax.axis_index("dp").astype(jnp.int32).reshape(1)
    return pl.pallas_call(
        output_kernel,
        grid_spec=pltpu.PrefetchScalarGridSpec(
            num_scalar_prefetch=1,
            grid=(count // block,),
            in_specs=[pl.BlockSpec((parts, block, units), lambda i, me: (0, i, 0))]
            + [pl.BlockSpec(d.shape, lambda i, me: (0, 0)) for d in down],
            out_specs=pl.BlockSpec((block, width), lambda i, me: (i, 0)),
        ),
        out_shape=jax.ShapeDtypeStruct((count, width), jnp.bfloat16),
        cost_estimate=pl.CostEstimate(
            flops=2 * parts * count * width * units,
            bytes_accessed=2 * parts * units * (count + width) + 2 * count * width,
            transcendentals=0,
        ),
        compiler_params=pltpu.CompilerParams(vmem_limit_bytes=48 << 20),
        name="output",
    )(me, hidden, *down)


def moments_kernel(chunks, count, *refs):
    gram_ref, project_ref = refs[-2:]
    first_ref = refs[0]
    gram = project = None
    for full_ref, own_ref in zip(refs[:chunks], refs[chunks : 2 * chunks]):
        rows = None
        for part in range(full_ref.shape[0]):
            basis = first_ref[part, count:, :]
            term = lax.dot_general(
                full_ref[part, :count, :],
                basis,
                (((1,), (1,)), ((), ())),
                preferred_element_type=jnp.float32,
            )
            rows = term if rows is None else rows + term
        turned = rows.T
        own = own_ref[:count, :].astype(jnp.float32)
        gram_term = jnp.dot(
            turned, rows, precision=lax.Precision.HIGHEST, preferred_element_type=jnp.float32
        )
        project_term = jnp.dot(
            turned, own, precision=lax.Precision.HIGHEST, preferred_element_type=jnp.float32
        )
        gram = gram_term if gram is None else gram + gram_term
        project = project_term if project is None else project + project_term
    size = gram.shape[0]
    row = lax.broadcasted_iota(jnp.int32, (size, size), 0)
    column = lax.broadcasted_iota(jnp.int32, (size, size), 1)
    gram_ref[...] = gram + jnp.where(row == column, ridge_term, 0.0)
    project_ref[...] = project


def moments(full, own, count, size):
    units = own[0].shape[1]
    return pl.pallas_call(
        functools.partial(moments_kernel, len(full), count),
        out_shape=[
            jax.ShapeDtypeStruct((size, size), jnp.float32),
            jax.ShapeDtypeStruct((size, units), jnp.float32),
        ],
        in_specs=[VMEM] * (2 * len(full)),
        out_specs=[VMEM] * 2,
        compiler_params=pltpu.CompilerParams(vmem_limit_bytes=48 << 20),
        name="moments",
    )(*full, *own)


def turn_down(down_weight, width):
    splits, me = lax.axis_size("dp"), lax.axis_index("dp")
    pieces = []
    for shift in range(splits):
        to = lax.rem(me + shift, splits)
        piece = lax.dynamic_slice_in_dim(down_weight, to * width, width, axis=1)
        if shift:
            piece = lax.ppermute(piece, "dp", [(i, (i + shift) % splits) for i in range(splits)])
        pieces.append(piece)
    return pieces


def body(tokens, routes, route_weights, gate_weight, up_weight, down_weight, sketch_basis):
    experts = lax.axis_size("expert")
    token_count, top = routes.shape
    capacity = 2 * token_count * top // experts
    chunks = SLOT_CHUNKS
    slots = capacity // chunks
    width = tokens.shape[1]
    rows = experts * slots

    down = turn_down(down_weight[0], width)
    basis = sketch_basis.T

    own, full, returned = [], [], []
    for chunk, outgoing in enumerate(dispatch(routes, tokens, experts, slots, chunks)):
        arrived = lax.all_to_all(
            outgoing.reshape(experts, slots, width), "expert", split_axis=0, concat_axis=0, tiled=True
        ).reshape(rows, width)
        if chunk == 0:
            arrived, *down = lax.optimization_barrier((arrived, *down))
        wide = lax.all_gather(arrived, "dp", axis=0, tiled=False)
        extra = (basis,) if chunk == 0 else ()
        hidden = hidden_of(wide, gate_weight[0], up_weight[0], extra)
        hidden_all = lax.all_gather(hidden, "dp", axis=0, tiled=False)
        out = output_of(hidden_all, down, rows)
        back = lax.all_to_all(
            out.reshape(experts, slots, width), "expert", split_axis=0, concat_axis=0, tiled=True
        ).reshape(rows, width)
        own.append(hidden)
        full.append(hidden_all)
        returned.append(back)
    gram, projected = moments(full, own, rows, basis.shape[0])
    lower_factor = jnp.linalg.cholesky(gram)
    whitened = jax.scipy.linalg.solve_triangular(lower_factor, projected, lower=True)
    mixed = combine(routes, route_weights, returned, experts, slots)
    return (mixed, whitened[None])


def solution(mesh):
    return jax.shard_map(
        body,
        mesh=mesh,
        in_specs=(
            P("expert", "dp"),
            P("expert", None),
            P("expert", None),
            P("expert", None, "dp"),
            P("expert", None, "dp"),
            P("expert", "dp", None),
            P("dp", None),
        ),
        out_specs=(P("expert", "dp"), P("expert", None, "dp")),
        check_vma=False,
    )
```

time: 464 us -> 301 us (0.65)
  waiting for transfers between devices: 321 us -> 191 us
  Pallas kernels: 0 us -> 29.8 us
  matrix products: 27.2 us -> 1.97 us
  local copies, waits for them, and re-layouts: 30.8 us -> 9.91 us
  other arithmetic: 33.6 us -> 23.7 us
  starting transfers between devices: 36.3 us -> 29.5 us
    all_to_all x3 -> x2, waiting for transfers between devices: 184 us -> 29.9 us  [the longest x1 18.9 us: body(): lax.all_to_all(out.reshape(experts, slots, width), 'expert', split_axis=0...]
    all_gather x1 -> x2, waiting for transfers between devices: 11.1 us -> 129 us  [the longest x1 82.1 us: body(): wide = lax.all_gather(arrived, 'dp', axis=0, tiled=False)]
    reduce_scatter x1 -> x0, waiting for transfers between devices: 78.8 us -> none  [body(): lax.psum_scatter(partial_value.reshape(owners, capacity, width).astype(jn...]
    psum x1 -> x0, waiting for transfers between devices: 45.9 us -> none  [body(): lax.psum(sketch_part.astype(jnp.bfloat16), 'dp').astype(jnp.float32)]
    ppermute x0 -> x3, waiting for transfers between devices: none -> 32.9 us  [turn_down(): lax.ppermute(piece, 'dp', [(i, (i + shift) % splits) for i in range(split...]
    pallas_call x0 -> x5, Pallas kernels: none -> 29.8 us  [the longest x1 13 us: hidden_of(): pl.pallas_call(hidden_kernel, grid=(count // block,), out_shape=jax.Shape...]
    dot_general x7 -> x0, matrix products: 26.1 us -> none  [the longest x1 7.97 us: body(): jnp.dot(slot_rows, gate_local, preferred_element_type=jnp.float32)]
    gather x2 -> x0, local copies, waits for them, and re-layouts: 21.8 us -> none  [the longest x1 16.4 us: body(): features[source_token].reshape(owners, capacity, features.shape[1])]
  transfers between devices with their start and end apart: 6 -> 7, of which waited for: 4 -> 6; matrix products, arithmetic and copies ran while one was open for 12% -> 10% of each run, Pallas kernels for 0% -> 1%
where the time goes in v1:
time: 301 us
  waiting for transfers between devices  191 us (63%)
  Pallas kernels  29.8 us (10%)
  starting transfers between devices  29.5 us (10%)
  other arithmetic  23.7 us (8%)
  between operations  14.2 us (5%)
  local copies, waits for them, and re-layouts  9.91 us (3%)
    all_gather x1, waiting for transfers between devices, body(): wide = lax.all_gather(arrived, 'dp', axis=0, tiled=False)  82.1 us
    all_gather x1, waiting for transfers between devices, body(): hidden_all = lax.all_gather(hidden, 'dp', axis=0, tiled=False)  46.5 us
    ppermute x3, waiting for transfers between devices, turn_down(): lax.ppermute(piece, 'dp', [(i, (i + shift) % splits) for i in range(split...  32.9 us
    all_to_all x1, waiting for transfers between devices, body(): lax.all_to_all(out.reshape(experts, slots, width), 'expert', split_axis=0...  18.9 us
    all_to_all x1, starting transfers between devices, body(): lax.all_to_all(outgoing.reshape(experts, slots, width), 'expert', split_a...  13.3 us
    pallas_call x1, Pallas kernels, hidden_of(): pl.pallas_call(hidden_kernel, grid=(count // block,), out_shape=jax.Shape...  13 us
    another operation x3, other arithmetic, body(): lower_factor = jnp.linalg.cholesky(gram)  12.4 us
    all_to_all x1, starting transfers between devices, body(): lax.all_to_all(out.reshape(experts, slots, width), 'expert', split_axis=0...  11.2 us
  transfers between devices with their start and end apart: 7, of which 6 were waited for; matrix products, arithmetic and copies ran while one was open for 10% of the time, Pallas kernels for 1%

profile of v1, /device:TPU:1, one launch (start us, length us, event | category | flops | bytes accessed | tf_op | source)
XLA Modules:
  0.0 300.6 jit_solution(8375165746775324917)
XLA Ops:
  7.2 1.4 copy.11.routes_ref
  8.6 3.5 %dispatch.1 = bf16[1024,1024]{1,0:T(8,128)(2,1)} custom-call(s32[128,4]{1,0:T(8,128)} %copy.11.routes_ref, bf16[128,1024]{1,0:T(8,128)(2,1)} %tokens_ref.1), custom_call_target="tpu_custom_call" | custom-call | tf_op jit(solution)/shard_map/dispatch/pallas_call | solution.py:52
  12.1 13.3 %all-to-all-start = ((bf16[64,16,1024]{2,1,0:T(8,128)(2,1)}), bf16[64,16,1024]{2,1,0:T(8,128)(2,1)}, u32[]{:S(2)}, u32[]{:S(2)}) async-start(bf16[64,16,1024]{2,1,0:T(8,128)(2,1)} %bitcast.35), calls=%async_computation | async-start | bytes 4194304 | tf_op jit(solution)/shard_map/all_to_all | solution.py:246
  25.4 0.0 all-gather.5.cloned.1.call-start
  25.5 0.0 copy-start.5
  25.5 2.2 dynamic-slice_bitcast_fusion
  27.7 1.3 collective-permute-start
  29.0 2.5 collective-permute-start.1
  31.5 1.1 collective-permute-start.2
  32.6 15.1 %collective-permute-done.refs_1_ = bf16[384,1024]{1,0:T(8,128)(2,1)S(1)} collective-permute-done((bf16[384,1024]{1,0:T(8,128)(2,1)S(1)}, bf16[384,1024]{1,0:T(8,128)(2,1)S(1)}, u32[]{:S(2)}, u32[]{:S(2)}) %collective-permute-start) | collective-permute-done | bytes 786464 | tf_op jit(solution)/shard_map/ppermute | solution.py:227
  47.7 17.8 %collective-permute-done.1.refs_2_ = bf16[384,1024]{1,0:T(8,128)(2,1)S(1)} collective-permute-done((bf16[384,1024]{1,0:T(8,128)(2,1)S(1)}, bf16[384,1024]{1,0:T(8,128)(2,1)S(1)}, u32[]{:S(2)}, u32[]{:S(2)}) %collective-permute-start.1) | collective-permute-done | bytes 786464 | tf_op jit(solution)/shard_map/ppermute | solution.py:227
  65.5 0.0 collective-permute-done.2.refs_3_
  65.5 11.0 %all-to-all-done = bf16[64,16,1024]{2,1,0:T(8,128)(2,1)} async-done(((bf16[64,16,1024]{2,1,0:T(8,128)(2,1)}), bf16[64,16,1024]{2,1,0:T(8,128)(2,1)}, u32[]{:S(2)}, u32[]{:S(2)}) %all-to-all-start) | async-done | bytes 2097184 | tf_op jit(solution)/shard_map/all_to_all | solution.py:246
  76.6 0.0 all-gather.5.cloned.1.call-update
  76.6 0.0 all-gather.7.cloned.1.call-start
  76.7 0.0 copy-done.5
  76.7 0.1 copy.10
  76.8 82.1 %all-gather.5.cloned.1.call-done = bf16[4096,1024]{1,0:T(8,128)(2,1)} async-done(((bf16[1024,1024]{1,0:T(8,128)(2,1)}), bf16[4096,1024]{1,0:T(8,128)(2,1)}) %all-gather.5.cloned.1.call-update) | async-done | bytes 8388624 | tf_op jit(solution)/shard_map/all_gather | solution.py:251
  158.9 0.0 copy-start.4
  158.9 1.9 copy-done.4
  160.8 13.0 %hidden.1.refs_1_ = bf16[1152,384]{1,0:T(8,128)(2,1)} custom-call(bf16[4,1024,1024]{2,1,0:T(8,128)(2,1)} %bitcast.36, bf16[4096,384]{1,0:T(8,128)(2,1)S(1)} %bitcast.34, bf16[4096,384]{1,0:T(8,128)(2,1)} %bitcast.37, bf16[128,384]{1,0:T(8,128)(2,1)S(1)} %bitcast.33), custom_call_target="tpu_custom_call" | custom-call | flops 6442450944 | bytes 15466496 | tf_op jit(solution)/shard_map/hidden/pallas_call | solution.py:120
  173.8 0.0 all-gather.7.cloned.1.call-update
  173.8 46.5 %all-gather.7.cloned.1.call-done = bf16[4608,384]{1,0:T(8,128)(2,1)} async-done(((bf16[1152,384]{1,0:T(8,128)(2,1)}), bf16[4608,384]{1,0:T(8,128)(2,1)}) %all-gather.7.cloned.1.call-update) | async-done | bytes 3538960 | tf_op jit(solution)/shard_map/all_gather | solution.py:254
  220.3 6.2 %output.1 = bf16[1024,1024]{1,0:T(8,128)(2,1)S(1)} custom-call(s32[1]{0:T(128)} %bitcast.me_ref, bf16[4,1152,384]{2,1,0:T(8,128)(2,1)} %bitcast.30, bf16[384,1024]{1,0:T(8,128)(2,1)S(1)} %get-tuple-element.10.refs_0_, bf16[384,1024]{1,0:T(8,128)(2,1)S(1)} %collective-permute-done.refs_1_, bf16[384,1024]{1,0:T(8,128)(2,1)S(1)} %collective-permute-done.1.refs_2_, ...), custom_call_target="tpu_custom_call" | custom-call | flops 3221225472 | bytes 8388608 | tf_op jit(solution)/shard_map/output/pallas_call | solution.py:153
  226.4 0.0 copy-start.1
  226.5 1.3 copy-done.1
  227.8 0.0 copy-start.6
  227.8 0.0 copy-start
  227.8 11.2 %all-to-all-start.1 = ((bf16[64,16,1024]{2,1,0:T(8,128)(2,1)}), bf16[64,16,1024]{2,1,0:T(8,128)(2,1)}, u32[]{:S(2)}, u32[]{:S(2)}) async-start(bf16[64,16,1024]{2,1,0:T(8,128)(2,1)} %bitcast.32), calls=%async_computation.1 | async-start | bytes 4194304 | tf_op jit(solution)/shard_map/all_to_all | solution.py:256
  238.9 0.0 copy-done.6
  238.9 0.7 copy.12.weights_ref
  239.7 0.0 copy-done
  239.7 3.5 %moments.1 = (f32[128,128]{1,0:T(8,128)S(1)}, f32[128,384]{1,0:T(8,128)S(1)}) custom-call(bf16[4,1152,384]{2,1,0:T(8,128)(2,1)S(1)} %bitcast.31, bf16[1152,384]{1,0:T(8,128)(2,1)} %hidden.1.refs_1_), custom_call_target="tpu_custom_call" | custom-call | tf_op jit(solution)/shard_map/moments/pallas_call | solution.py:207
  243.2 0.0 copy-start.2
  243.3 0.6 copy-done.2
  243.9 0.0 copy-start.3
  243.9 0.7 copy-done.3
  244.5 0.9 copy.13
  245.5 0.9 fusion.2
  246.3 11.7 %cholesky.16 = f32[128,128]{1,0:T(8,128)S(1)} custom-call(f32[128,128]{1,0:T(8,128)S(1)} %fusion.2), custom_call_target="Cholesky" | custom-call | tf_op jit(solution)/shard_map/jit(cholesky)/cholesky | solution.py:263
  258.1 0.6 compare_reduce_fusion
  258.7 0.7 fusion
  259.4 9.8 %custom-call.7 = f32[1,128,128]{1,2,0:T(8,128)S(1)} custom-call(f32[1,128,128]{2,1,0:T(8,128)S(1)} %fusion), custom_call_target="InvertDiagBlocksLowerTriangular" | custom-call | tf_op jit(solution)/shard_map/jit(_solve_triangular)/triangular_solve | solution.py:264
  269.2 2.0 convolution_bitcast_fusion
  271.2 18.9 %all-to-all-done.1 = bf16[64,16,1024]{2,1,0:T(8,128)(2,1)} async-done(((bf16[64,16,1024]{2,1,0:T(8,128)(2,1)}), bf16[64,16,1024]{2,1,0:T(8,128)(2,1)}, u32[]{:S(2)}, u32[]{:S(2)}) %all-to-all-start.1) | async-done | bytes 2097184 | tf_op jit(solution)/shard_map/all_to_all | solution.py:256
  290.1 3.6 %combine.1 = bf16[128,1024]{1,0:T(8,128)(2,1)} custom-call(s32[128,4]{1,0:T(8,128)} %copy.11.routes_ref, f32[128,4]{1,0:T(8,128)} %copy.12.weights_ref, bf16[1024,1024]{1,0:T(8,128)(2,1)} %bitcast.13.refs_0_), custom_call_target="tpu_custom_call" | custom-call | tf_op jit(solution)/shard_map/combine/pallas_call | solution.py:84
  (1 shorter events, 0.0 us)
Async XLA Ops:
  12.1 64.5 %all-to-all-start = ((bf16[64,16,1024]{2,1,0:T(8,128)(2,1)}), bf16[64,16,1024]{2,1,0:T(8,128)(2,1)}, u32[]{:S(2)}, u32[]{:S(2)}) async-start(bf16[64,16,1024]{2,1,0:T(8,128)(2,1)} %bitcast.35), calls=%async_computation | async-start | bytes 4194304 | tf_op jit(solution)/shard_map/all_to_all | solution.py:246
  25.4 133.5 %all-gather.5.cloned.1.call-start = ((), (), s32[]{:S(2)}) async-start(), calls=%async_computation.2 | async-start | bytes 10485760 | tf_op jit(solution)/shard_map/all_gather | solution.py:251
  25.5 51.2 %copy-start.5 = (bf16[384,128]{1,0:T(8,128)(2,1)S(1)}, bf16[384,128]{1,0:T(8,128)(2,1)}, u32[]{:S(2)}) copy-start(bf16[384,128]{1,0:T(8,128)(2,1)} %param.13) | copy-start | bytes 294916
  27.7 20.0 %collective-permute-start = (bf16[384,1024]{1,0:T(8,128)(2,1)S(1)}, bf16[384,1024]{1,0:T(8,128)(2,1)S(1)}, u32[]{:S(2)}, u32[]{:S(2)}) collective-permute-start(bf16[384,1024]{1,0:T(8,128)(2,1)S(1)} %get-tuple-element.17), channel_id=1, source_target_pairs={{0,64},{64,128},{128,192},{192,0},{1,65},{65,129},{129,193},{193,1... | collective-permute-start | bytes 2359304 | tf_op jit(solution)/shard_map/ppermute | solution.py:227
  29.0 36.5 %collective-permute-start.1 = (bf16[384,1024]{1,0:T(8,128)(2,1)S(1)}, bf16[384,1024]{1,0:T(8,128)(2,1)S(1)}, u32[]{:S(2)}, u32[]{:S(2)}) collective-permute-start(bf16[384,1024]{1,0:T(8,128)(2,1)S(1)} %get-tuple-element.19), channel_id=1, source_target_pairs={{0,128},{64,192},{128,0},{192,64},{1,129},{65,193},{129,1},{193,65... | collective-permute-start | bytes 2359304 | tf_op jit(solution)/shard_map/ppermute | solution.py:227
  31.5 34.1 %collective-permute-start.2 = (bf16[384,1024]{1,0:T(8,128)(2,1)S(1)}, bf16[384,1024]{1,0:T(8,128)(2,1)S(1)}, u32[]{:S(2)}, u32[]{:S(2)}) collective-permute-start(bf16[384,1024]{1,0:T(8,128)(2,1)S(1)} %get-tuple-element.16), channel_id=1, source_target_pairs={{0,192},{64,0},{128,64},{192,128},{1,193},{65,1},{129,65},{193,129... | collective-permute-start | bytes 2359304 | tf_op jit(solution)/shard_map/ppermute | solution.py:227
  76.6 143.7 %all-gather.7.cloned.1.call-start = ((), (), s32[]{:S(2)}) async-start(), calls=%async_computation.3 | async-start | bytes 4423680 | tf_op jit(solution)/shard_map/all_gather | solution.py:254
  158.9 1.9 copy-start.4
  226.4 1.3 copy-start.1
  227.8 11.2 %copy-start.6 = (f32[128,4]{0,1:T(4,128)S(1)}, f32[128,4]{0,1:T(4,128)}, u32[]{:S(2)}) copy-start(f32[128,4]{0,1:T(4,128)} %param.9) | copy-start | bytes 6148
  227.8 11.9 %copy-start = (bf16[4608,384]{1,0:T(8,128)(2,1)S(1)}, bf16[4608,384]{1,0:T(8,128)(2,1)}, u32[]{:S(2)}) copy-start(bf16[4608,384]{1,0:T(8,128)(2,1)} %all-gather.7.cloned.1.call-done) | copy-start | bytes 10616836
  227.8 62.3 %all-to-all-start.1 = ((bf16[64,16,1024]{2,1,0:T(8,128)(2,1)}), bf16[64,16,1024]{2,1,0:T(8,128)(2,1)}, u32[]{:S(2)}, u32[]{:S(2)}) async-start(bf16[64,16,1024]{2,1,0:T(8,128)(2,1)} %bitcast.32), calls=%async_computation.1 | async-start | bytes 4194304 | tf_op jit(solution)/shard_map/all_to_all | solution.py:256
  243.2 0.6 copy-start.2
  243.9 0.7 copy-start.3
Sparse Core Ops, SparseCore 0:
  76.7 82.1 all-gather.4
  173.9 46.3 all-gather.6

commit v2 on v1

v2 whole, which is shorter than its diff:
```python
import functools

import jax
import jax.numpy as jnp
from jax import lax
from jax.experimental import pallas as pl
from jax.experimental.pallas import tpu as pltpu
from jax.sharding import PartitionSpec as P

ridge_term = 1.0
CUTS = (8, 8)
VMEM = pl.BlockSpec(memory_space=pltpu.VMEM)


def slot_codes(routes, experts):
    tokens, top = routes.shape
    expert_of = lax.broadcasted_iota(jnp.int32, (tokens, experts), 1)
    hits = [(routes[:, k : k + 1] == expert_of).astype(jnp.float32) for k in range(top)]
    hit = functools.reduce(jnp.add, hits)
    row = lax.broadcasted_iota(jnp.int32, (tokens, tokens), 0)
    column = lax.broadcasted_iota(jnp.int32, (tokens, tokens), 1)
    earlier = (row > column).astype(jnp.bfloat16)
    before = jnp.dot(earlier, hit.astype(jnp.bfloat16), preferred_element_type=jnp.float32)
    return hits, jnp.where(hit > 0.0, before, -1.0)


def spread(values, experts, slots):
    expert = lax.broadcasted_iota(jnp.int32, (experts, experts * slots), 0)
    at = lax.broadcasted_iota(jnp.int32, (experts, experts * slots), 1)
    ones = jnp.where(at // slots == expert, 1.0, 0.0).astype(jnp.bfloat16)
    return jnp.dot(values.astype(jnp.bfloat16), ones, preferred_element_type=jnp.float32)


def in_slot(code, experts, slots, start):
    wide = spread(code, experts, slots)
    at = lax.broadcasted_iota(jnp.int32, wide.shape, 1)
    return wide == (lax.rem(at, slots) + start).astype(jnp.float32)


def dispatch_kernel(experts, cuts, routes_ref, tokens_ref, *out_refs):
    _, code = slot_codes(routes_ref[...], experts)
    tokens = tokens_ref[...]
    start = 0
    for slots, out_ref in zip(cuts, out_refs):
        chosen = jnp.where(in_slot(code, experts, slots, start), 1.0, 0.0).T.astype(jnp.bfloat16)
        out_ref[...] = jnp.dot(chosen, tokens, preferred_element_type=jnp.float32).astype(out_ref.dtype)
        start += slots


def dispatch(routes, tokens, experts, cuts):
    width = tokens.shape[1]
    return pl.pallas_call(
        functools.partial(dispatch_kernel, experts, cuts),
        out_shape=[jax.ShapeDtypeStruct((experts * slots, width), tokens.dtype) for slots in cuts],
        in_specs=[VMEM] * 2,
        out_specs=[VMEM] * len(cuts),
        name="dispatch",
    )(routes, tokens)


def combine_kernel(experts, cuts, routes_ref, weights_ref, *refs):
    out_ref = refs[-1]
    hits, code = slot_codes(routes_ref[...], experts)
    weights = weights_ref[...]
    weight = functools.reduce(jnp.add, [h * weights[:, k : k + 1] for k, h in enumerate(hits)])
    high = weight.astype(jnp.bfloat16)
    low = (weight - high.astype(jnp.float32)).astype(jnp.bfloat16)
    total = None
    start = 0
    for slots, row_ref in zip(cuts, refs[:-1]):
        chosen = in_slot(code, experts, slots, start)
        rows = row_ref[...]
        for part in (high, low):
            matrix = jnp.where(chosen, spread(part, experts, slots), 0.0).astype(jnp.bfloat16)
            term = jnp.dot(matrix, rows, preferred_element_type=jnp.float32)
            total = term if total is None else total + term
        start += slots
    out_ref[...] = total.astype(out_ref.dtype)


def combine(routes, weights, rows, experts, cuts):
    return pl.pallas_call(
        functools.partial(combine_kernel, experts, cuts),
        out_shape=jax.ShapeDtypeStruct((routes.shape[0], rows[0].shape[1]), jnp.bfloat16),
        in_specs=[VMEM] * (2 + len(rows)),
        out_specs=VMEM,
        name="combine",
    )(routes, weights, *rows)


def hidden_kernel(me_ref, own_ref, left_ref, right_ref, top_ref, bottom_ref, gate_ref, up_ref, hidden_ref):
    width = own_ref.shape[1]
    parts = gate_ref.shape[0] // width
    step = pl.program_id(0)
    far = jnp.where(step == 0, top_ref[...], bottom_ref[...])
    gate = up = None
    for shift, rows in ((0, own_ref[...]), (parts - 1, left_ref[...]), (1, right_ref[...]), (2, far)):
        at = pl.multiple_of(lax.rem(me_ref[0] + shift, parts) * width, width)
        gate_term = jnp.dot(rows, gate_ref[pl.ds(at, width), :], preferred_element_type=jnp.float32)
        up_term = jnp.dot(rows, up_ref[pl.ds(at, width), :], preferred_element_type=jnp.float32)
        gate = gate_term if gate is None else gate + gate_term
        up = up_term if up is None else up + up_term
    hidden_ref[...] = (gate / (1.0 + jnp.exp(-gate)) * up).astype(hidden_ref.dtype)


def hidden_of(me, ring, gate_weight, up_weight):
    own, left, right, top, bottom = ring
    count, width = own.shape
    depth, units = gate_weight.shape
    half = count // 2
    rows = pl.BlockSpec((half, width), lambda i, me: (i, 0))
    fixed = pl.BlockSpec((half, width), lambda i, me: (0, 0))
    whole = pl.BlockSpec((depth, units), lambda i, me: (0, 0))
    return pl.pallas_call(
        hidden_kernel,
        grid_spec=pltpu.PrefetchScalarGridSpec(
            num_scalar_prefetch=1,
            grid=(2,),
            in_specs=[rows, rows, rows, fixed, fixed, whole, whole],
            out_specs=pl.BlockSpec((half, units), lambda i, me: (i, 0)),
        ),
        out_shape=jax.ShapeDtypeStruct((count, units), jnp.bfloat16),
        cost_estimate=pl.CostEstimate(
            flops=4 * count * depth * units,
            bytes_accessed=2 * depth * (count + 2 * units) + 2 * count * units,
            transcendentals=count * units,
        ),
        compiler_params=pltpu.CompilerParams(vmem_limit_bytes=48 << 20),
        name="hidden",
    )(me, own, left, right, top, bottom, gate_weight, up_weight)


def output_kernel(parts, *refs):
    out_ref, sketch_ref = refs[-2:]
    width = out_ref.shape[1]
    total = None
    for hidden_ref, down_ref in zip(refs[:parts], refs[parts : 2 * parts]):
        term = jnp.dot(hidden_ref[...], down_ref[...], preferred_element_type=jnp.float32)
        total = term if total is None else total + term
    out_ref[...] = total[:, :width].astype(out_ref.dtype)
    sketch_ref[...] = total[:, width:]


def output_of(hidden, down, width):
    count, units = hidden[0].shape
    parts, wide = len(hidden), down[0].shape[1]
    block = count // 2
    return pl.pallas_call(
        functools.partial(output_kernel, parts),
        grid=(count // block,),
        in_specs=[pl.BlockSpec((block, units), lambda i: (i, 0))] * parts
        + [pl.BlockSpec((units, wide), lambda i: (0, 0))] * parts,
        out_specs=[
            pl.BlockSpec((block, width), lambda i: (i, 0)),
            pl.BlockSpec((block, wide - width), lambda i: (i, 0)),
        ],
        out_shape=[
            jax.ShapeDtypeStruct((count, width), jnp.bfloat16),
            jax.ShapeDtypeStruct((count, wide - width), jnp.float32),
        ],
        cost_estimate=pl.CostEstimate(
            flops=2 * parts * count * wide * units,
            bytes_accessed=2 * parts * units * (count + wide) + 4 * count * wide,
            transcendentals=0,
        ),
        compiler_params=pltpu.CompilerParams(vmem_limit_bytes=48 << 20),
        name="output",
    )(*hidden, *down)


def moments_kernel(chunks, *refs):
    gram_ref, project_ref = refs[-2:]
    gram = project = None
    for rows_ref, own_ref in zip(refs[:chunks], refs[chunks : 2 * chunks]):
        rows = rows_ref[...]
        turned = rows.T
        own = own_ref[...].astype(jnp.float32)
        gram_term = jnp.dot(
            turned, rows, precision=lax.Precision.HIGHEST, preferred_element_type=jnp.float32
        )
        project_term = jnp.dot(
            turned, own, precision=lax.Precision.HIGHEST, preferred_element_type=jnp.float32
        )
        gram = gram_term if gram is None else gram + gram_term
        project = project_term if project is None else project + project_term
    size = gram.shape[0]
    row = lax.broadcasted_iota(jnp.int32, (size, size), 0)
    column = lax.broadcasted_iota(jnp.int32, (size, size), 1)
    gram_ref[...] = gram + jnp.where(row == column, ridge_term, 0.0)
    project_ref[...] = project


def moments(rows, own):
    size, units = rows[0].shape[1], own[0].shape[1]
    return pl.pallas_call(
        functools.partial(moments_kernel, len(rows)),
        out_shape=[
            jax.ShapeDtypeStruct((size, size), jnp.float32),
            jax.ShapeDtypeStruct((size, units), jnp.float32),
        ],
        in_specs=[VMEM] * (2 * len(rows)),
        out_specs=[VMEM] * 2,
        compiler_params=pltpu.CompilerParams(vmem_limit_bytes=48 << 20),
        name="moments",
    )(*rows, *own)


def shift_by(value, shift):
    splits = lax.axis_size("dp")
    return lax.ppermute(value, "dp", [(i, (i + shift) % splits) for i in range(splits)])


def turn_down(down_weight, basis, width):
    splits, me = lax.axis_size("dp"), lax.axis_index("dp")
    pieces = []
    for shift in range(splits):
        to = lax.rem(me + shift, splits)
        piece = lax.dynamic_slice_in_dim(down_weight, to * width, width, axis=1)
        piece = jnp.concatenate([piece, basis], axis=1)
        pieces.append(shift_by(piece, shift) if shift else piece)
    return pieces


def around(own):
    half = own.shape[0] // 2
    left, right = shift_by(own, 1), shift_by(own, -1)
    return own, left, right, shift_by(left[:half], 1), shift_by(right[half:], -1)


def body(tokens, routes, route_weights, gate_weight, up_weight, down_weight, sketch_basis):
    experts = lax.axis_size("expert")
    token_count, top = routes.shape
    capacity = 2 * token_count * top // experts
    width = tokens.shape[1]
    me = lax.axis_index("dp").astype(jnp.int32).reshape(1)

    def swap(rows):
        blocks = rows.reshape(experts, rows.shape[0] // experts, width)
        return lax.all_to_all(blocks, "expert", split_axis=0, concat_axis=0, tiled=True).reshape(rows.shape)

    down = turn_down(down_weight[0], sketch_basis, width)
    own, sketch_rows, returned = [], [], []
    for outgoing in dispatch(routes, tokens, experts, CUTS):
        arrived = swap(outgoing)
        if not own:
            arrived, down[1], down[3] = lax.optimization_barrier((arrived, down[1], down[3]))
        hidden = hidden_of(me, around(arrived), gate_weight[0], up_weight[0])
        everywhere = [hidden] + [shift_by(hidden, s) for s in range(1, lax.axis_size("dp"))]
        out, rows = output_of(everywhere, down, width)
        own.append(hidden)
        sketch_rows.append(rows)
        returned.append(swap(out))
    gram, projected = moments(sketch_rows, own)
    lower_factor = jnp.linalg.cholesky(gram)
    whitened = jax.scipy.linalg.solve_triangular(lower_factor, projected, lower=True)
    mixed = combine(routes, route_weights, returned, experts, CUTS)
    return (mixed, whitened[None])


def solution(mesh):
    return jax.shard_map(
        body,
        mesh=mesh,
        in_specs=(
            P("expert", "dp"),
            P("expert", None),
            P("expert", None),
            P("expert", None, "dp"),
            P("expert", None, "dp"),
            P("expert", "dp", None),
            P("dp", None),
        ),
        out_specs=(P("expert", "dp"), P("expert", None, "dp")),
        check_vma=False,
    )
```

time: 301 us -> 258 us (0.86)
  waiting for transfers between devices: 191 us -> 92.6 us
  blocking collectives: 0 us -> 41.7 us
  starting transfers between devices: 29.5 us -> 48.9 us
  between operations: 14.2 us -> 0.86 us
  Pallas kernels: 29.8 us -> 33.9 us
  local copies, waits for them, and re-layouts: 9.91 us -> 13.9 us
    all_gather x2 -> x0, waiting for transfers between devices: 129 us -> none  [the longest x1 82.1 us: body(): wide = lax.all_gather(arrived, 'dp', axis=0, tiled=False)]
    ppermute x3 -> x17, waiting for transfers between devices: 32.9 us -> 90.3 us  [shift_by(): lax.ppermute(value, 'dp', [(i, (i + shift) % splits) for i in range(split...]
    all_to_all x0 -> x1, blocking collectives: none -> 41.7 us  [swap(): lax.all_to_all(blocks, 'expert', split_axis=0, concat_axis=0, tiled=True)]
    all_to_all x2 -> x3, waiting for transfers between devices: 29.9 us -> 2.28 us  [swap(): lax.all_to_all(blocks, 'expert', split_axis=0, concat_axis=0, tiled=True)]
    ppermute x3 -> x17, starting transfers between devices: 4.89 us -> 22.5 us  [shift_by(): lax.ppermute(value, 'dp', [(i, (i + shift) % splits) for i in range(split...]
    slice x0 -> x4, local copies, waits for them, and re-layouts: none -> 4.31 us  [the longest x2 2.15 us: around(): left[:half]]
    pallas_call x5 -> x7, Pallas kernels: 29.8 us -> 33.9 us  [the longest x2 15.8 us: hidden_of(): pl.pallas_call(hidden_kernel, grid_spec=pltpu.PrefetchScalarGridSpec(num_...]
    all_to_all x2 -> x3, starting transfers between devices: 24.5 us -> 26.4 us  [swap(): lax.all_to_all(blocks, 'expert', split_axis=0, concat_axis=0, tiled=True)]
  transfers between devices with their start and end apart: 7 -> 20, of which waited for: 6 -> 13; matrix products, arithmetic and copies ran while one was open for 10% -> 13% of each run, Pallas kernels for 1% -> 11%
where the time goes in v2:
time: 258 us; the launch traced here: 257 us
  waiting for transfers between devices  92.6 us (36%)
  starting transfers between devices  48.9 us (19%)
  blocking collectives  41.7 us (16%)
  Pallas kernels  33.9 us (13%)
  other arithmetic  24.1 us (9%)
  local copies, waits for them, and re-layouts  13.9 us (5%)
    ppermute x17, waiting for transfers between devices, shift_by(): lax.ppermute(value, 'dp', [(i, (i + shift) % splits) for i in range(split...  90.3 us
    all_to_all x1, blocking collectives, swap(): lax.all_to_all(blocks, 'expert', split_axis=0, concat_axis=0, tiled=True)  41.7 us
    all_to_all x3, starting transfers between devices, swap(): lax.all_to_all(blocks, 'expert', split_axis=0, concat_axis=0, tiled=True)  26.4 us
    ppermute x17, starting transfers between devices, shift_by(): lax.ppermute(value, 'dp', [(i, (i + shift) % splits) for i in range(split...  22.5 us
    pallas_call x2, Pallas kernels, hidden_of(): pl.pallas_call(hidden_kernel, grid_spec=pltpu.PrefetchScalarGridSpec(num_...  15.8 us
    another operation x3, other arithmetic, body(): lower_factor = jnp.linalg.cholesky(gram)  12.4 us
    another operation x2, other arithmetic, body(): jax.scipy.linalg.solve_triangular(lower_factor, projected, lower=True)  10.5 us
    pallas_call x2, Pallas kernels, output_of(): pl.pallas_call(functools.partial(output_kernel, parts), grid=(count // bl...  9.81 us
  transfers between devices with their start and end apart: 20, of which 13 were waited for; matrix products, arithmetic and copies ran while one was open for 13% of the time, Pallas kernels for 11%

profile of v2, /device:TPU:1, one launch (start us, length us, event | category | flops | bytes accessed | tf_op | source)
XLA Modules:
  0.0 257.1 jit_solution(4826964272283513977)
XLA Ops:
  0.6 1.4 copy.10.routes_ref
  2.0 3.2 %dispatch.1 = (bf16[512,1024]{1,0:T(8,128)(2,1)}, bf16[512,1024]{1,0:T(8,128)(2,1)}) custom-call(s32[128,4]{1,0:T(8,128)} %copy.10.routes_ref, bf16[128,1024]{1,0:T(8,128)(2,1)} %tokens_ref.1), custom_call_target="tpu_custom_call" | custom-call | tf_op jit(solution)/shard_map/dispatch/pallas_call | solution.py:52
  5.3 41.7 %all_to_all.20 = bf16[64,8,1024]{2,1,0:T(8,128)(2,1)S(1)} all-to-all(bf16[64,8,1024]{2,1,0:T(8,128)(2,1)} %bitcast.40), channel_id=1, replica_groups=mesh['dp'=4,'expert'=64] {'expert'}, dimensions={0} | all-to-all | bytes 2097152 | tf_op jit(solution)/shard_map/all_to_all | solution.py:239
  47.0 1.2 collective-permute-start.10
  48.2 1.5 collective-permute-start.11
  49.7 6.7 %all-to-all-start = ((bf16[64,8,1024]{2,1,0:T(8,128)(2,1)}), bf16[64,8,1024]{2,1,0:T(8,128)(2,1)S(1)}, u32[]{:S(2)}, u32[]{:S(2)}) async-start(bf16[64,8,1024]{2,1,0:T(8,128)(2,1)} %bitcast.1), calls=%async_computation | async-start | bytes 2097152 | tf_op jit(solution)/shard_map/all_to_all | solution.py:239
  56.5 2.2 dynamic-slice_bitcast_fusion
  58.7 1.3 pad_maximum_fusion
  60.0 13.0 %collective-permute-done.10.left_ref = bf16[512,1024]{1,0:T(8,128)(2,1)} collective-permute-done((bf16[512,1024]{1,0:T(8,128)(2,1)S(1)}, bf16[512,1024]{1,0:T(8,128)(2,1)}, u32[]{:S(2)}, u32[]{:S(2)}) %collective-permute-start.10) | collective-permute-done | bytes 1048608 | tf_op jit(solution)/shard_map/ppermute | solution.py:210
  73.0 1.1 slice.30
  74.2 1.1 slice.31
  75.3 2.7 %collective-permute-start.13 = (bf16[256,1024]{1,0:T(8,128)(2,1)S(1)}, bf16[256,1024]{1,0:T(8,128)(2,1)S(1)}, u32[]{:S(2)}, u32[]{:S(2)}) collective-permute-start(bf16[256,1024]{1,0:T(8,128)(2,1)S(1)} %slice.31), channel_id=1, source_target_pairs={{0,192},{64,0},{128,64},{192,128},{1,193},{65,1},{129,65},{193,129... | collective-permute-start | bytes 1572872 | tf_op jit(solution)/shard_map/ppermute | solution.py:210
  78.6 24.5 %collective-permute-done.12.top_ref = bf16[256,1024]{1,0:T(8,128)(2,1)S(1)} collective-permute-done((bf16[256,1024]{1,0:T(8,128)(2,1)S(1)}, bf16[256,1024]{1,0:T(8,128)(2,1)S(1)}, u32[]{:S(2)}, u32[]{:S(2)}) %collective-permute-start.12) | collective-permute-done | bytes 524320 | tf_op jit(solution)/shard_map/ppermute | solution.py:210
  103.1 7.9 %hidden.3.refs_0_.refs_3_ = bf16[512,384]{1,0:T(8,128)(2,1)S(1)} custom-call(s32[1]{0:T(128)} %bitcast.me_ref, bf16[512,1024]{1,0:T(8,128)(2,1)S(1)} %bitcast.36, bf16[512,1024]{1,0:T(8,128)(2,1)} %collective-permute-done.10.left_ref, bf16[512,1024]{1,0:T(8,128)(2,1)} %collective-permute-done.11.right_ref, ...), custom_call_target="tpu_custom_call" | custom-call | flops 3221225472 | bytes 10878976 | tf_op jit(solution)/shard_map/hidden/pallas_call | solution.py:114
  111.2 2.4 collective-permute-start.15
  113.6 0.9 copy-done
  114.5 1.2 collective-permute-start.16
  115.7 0.9 copy-done.3
  116.9 6.3 %collective-permute-done.9.refs_6_ = bf16[384,1152]{1,0:T(8,128)(2,1)} collective-permute-done((bf16[384,1152]{1,0:T(8,128)(2,1)}, bf16[384,1152]{1,0:T(8,128)(2,1)}, u32[]{:S(2)}, u32[]{:S(2)}) %collective-permute-start.9) | collective-permute-done | bytes 884768 | tf_op jit(solution)/shard_map/ppermute | solution.py:210
  123.2 4.5 %collective-permute-start.3 = (bf16[512,1024]{1,0:T(8,128)(2,1)S(1)}, bf16[512,1024]{1,0:T(8,128)(2,1)}, u32[]{:S(2)}, u32[]{:S(2)}) collective-permute-start(bf16[512,1024]{1,0:T(8,128)(2,1)S(1)} %bitcast.32), channel_id=1, source_target_pairs={{0,192},{64,0},{128,64},{192,128},{1,193},{65,1},{129,65},{193,129... | collective-permute-start | bytes 3145736 | tf_op jit(solution)/shard_map/ppermute | solution.py:210
  127.7 4.5 %collective-permute-done.14.refs_1_ = bf16[512,384]{1,0:T(8,128)(2,1)S(1)} collective-permute-done((bf16[512,384]{1,0:T(8,128)(2,1)S(1)}, bf16[512,384]{1,0:T(8,128)(2,1)S(1)}, u32[]{:S(2)}, u32[]{:S(2)}) %collective-permute-start.14) | collective-permute-done | bytes 393248 | tf_op jit(solution)/shard_map/ppermute | solution.py:210
  132.2 7.8 %collective-permute-done.15.refs_2_ = bf16[512,384]{1,0:T(8,128)(2,1)S(1)} collective-permute-done((bf16[512,384]{1,0:T(8,128)(2,1)S(1)}, bf16[512,384]{1,0:T(8,128)(2,1)S(1)}, u32[]{:S(2)}, u32[]{:S(2)}) %collective-permute-start.15) | collective-permute-done | bytes 393248 | tf_op jit(solution)/shard_map/ppermute | solution.py:210
  140.0 3.2 %collective-permute-done.16.refs_3_ = bf16[512,384]{1,0:T(8,128)(2,1)} collective-permute-done((bf16[512,384]{1,0:T(8,128)(2,1)S(1)}, bf16[512,384]{1,0:T(8,128)(2,1)}, u32[]{:S(2)}, u32[]{:S(2)}) %collective-permute-start.16) | collective-permute-done | bytes 393248 | tf_op jit(solution)/shard_map/ppermute | solution.py:210
  143.2 1.2 copy-done.1
  144.4 1.2 copy-done.4
  145.6 5.0 %output.3 = (bf16[512,1024]{1,0:T(8,128)(2,1)}, f32[512,128]{1,0:T(8,128)S(1)}) custom-call(bf16[512,384]{1,0:T(8,128)(2,1)S(1)} %hidden.3.refs_0_.refs_3_, bf16[512,384]{1,0:T(8,128)(2,1)S(1)} %collective-permute-done.14.refs_1_, bf16[512,384]{1,0:T(8,128)(2,1)S(1)} %collective-permute-done.15.refs_2_, bf16[512,384]{1,0:T(8,128)(2,1)} %collective-permute-done.16.refs_3_, ...), custom_call_target="tpu_custom_call" | custom-call | flops 1811939328 | bytes 7471104 | tf_op jit(solution)/shard_map/output/pallas_call | solution.py:148
  150.5 9.9 %all-to-all-start.3 = ((bf16[64,8,1024]{2,1,0:T(8,128)(2,1)}), bf16[64,8,1024]{2,1,0:T(8,128)(2,1)}, u32[]{:S(2)}, u32[]{:S(2)}) async-start(bf16[64,8,1024]{2,1,0:T(8,128)(2,1)} %bitcast.38), calls=%async_computation.3 | async-start | bytes 2097152 | tf_op jit(solution)/shard_map/all_to_all | solution.py:239
  160.5 1.1 slice.28
  162.0 3.7 %collective-permute-done.3.right_ref = bf16[512,1024]{1,0:T(8,128)(2,1)} collective-permute-done((bf16[512,1024]{1,0:T(8,128)(2,1)S(1)}, bf16[512,1024]{1,0:T(8,128)(2,1)}, u32[]{:S(2)}, u32[]{:S(2)}) %collective-permute-start.3) | collective-permute-done | bytes 1048608 | tf_op jit(solution)/shard_map/ppermute | solution.py:210
  165.7 1.1 slice.29
  166.8 3.6 %collective-permute-start.5 = (bf16[256,1024]{1,0:T(8,128)(2,1)S(1)}, bf16[256,1024]{1,0:T(8,128)(2,1)S(1)}, u32[]{:S(2)}, u32[]{:S(2)}) collective-permute-start(bf16[256,1024]{1,0:T(8,128)(2,1)S(1)} %slice.29), channel_id=1, source_target_pairs={{0,192},{64,0},{128,64},{192,128},{1,193},{65,1},{129,65},{193,129... | collective-permute-start | bytes 1572872 | tf_op jit(solution)/shard_map/ppermute | solution.py:210
  170.4 3.2 %collective-permute-done.4.top_ref = bf16[256,1024]{1,0:T(8,128)(2,1)S(1)} collective-permute-done((bf16[256,1024]{1,0:T(8,128)(2,1)S(1)}, bf16[256,1024]{1,0:T(8,128)(2,1)S(1)}, u32[]{:S(2)}, u32[]{:S(2)}) %collective-permute-start.4) | collective-permute-done | bytes 524320 | tf_op jit(solution)/shard_map/ppermute | solution.py:210
  173.6 7.6 %collective-permute-done.5.bottom_ref = bf16[256,1024]{1,0:T(8,128)(2,1)S(1)} collective-permute-done((bf16[256,1024]{1,0:T(8,128)(2,1)S(1)}, bf16[256,1024]{1,0:T(8,128)(2,1)S(1)}, u32[]{:S(2)}, u32[]{:S(2)}) %collective-permute-start.5) | collective-permute-done | bytes 524320 | tf_op jit(solution)/shard_map/ppermute | solution.py:210
  181.2 7.9 %hidden.2.refs_0_.refs_2_ = bf16[512,384]{1,0:T(8,128)(2,1)S(1)} custom-call(s32[1]{0:T(128)} %bitcast.me_ref, bf16[512,1024]{1,0:T(8,128)(2,1)S(1)} %bitcast.33, bf16[512,1024]{1,0:T(8,128)(2,1)} %collective-permute-done.2.left_ref, bf16[512,1024]{1,0:T(8,128)(2,1)} %collective-permute-done.3.right_ref, ...), custom_call_target="tpu_custom_call" | custom-call | flops 3221225472 | bytes 10878976 | tf_op jit(solution)/shard_map/hidden/pallas_call | solution.py:114
  189.2 1.5 collective-permute-start.6
  190.7 1.9 collective-permute-start.7
  193.2 6.2 %collective-permute-done.6.refs_1_ = bf16[512,384]{1,0:T(8,128)(2,1)S(1)} collective-permute-done((bf16[512,384]{1,0:T(8,128)(2,1)S(1)}, bf16[512,384]{1,0:T(8,128)(2,1)S(1)}, u32[]{:S(2)}, u32[]{:S(2)}) %collective-permute-start.6) | collective-permute-done | bytes 393248 | tf_op jit(solution)/shard_map/ppermute | solution.py:210
  199.3 8.3 %collective-permute-done.7.refs_2_ = bf16[512,384]{1,0:T(8,128)(2,1)S(1)} collective-permute-done((bf16[512,384]{1,0:T(8,128)(2,1)S(1)}, bf16[512,384]{1,0:T(8,128)(2,1)S(1)}, u32[]{:S(2)}, u32[]{:S(2)}) %collective-permute-start.7) | collective-permute-done | bytes 393248 | tf_op jit(solution)/shard_map/ppermute | solution.py:210
  207.7 1.8 collective-permute-done.8.refs_3_
  209.5 4.8 %output.2 = (bf16[512,1024]{1,0:T(8,128)(2,1)}, f32[512,128]{1,0:T(8,128)S(1)}) custom-call(bf16[512,384]{1,0:T(8,128)(2,1)S(1)} %hidden.2.refs_0_.refs_2_, bf16[512,384]{1,0:T(8,128)(2,1)S(1)} %collective-permute-done.6.refs_1_, bf16[512,384]{1,0:T(8,128)(2,1)S(1)} %collective-permute-done.7.refs_2_, bf16[512,384]{1,0:T(8,128)(2,1)S(1)} %collective-permute-done.8.refs_3_, ...), custom_call_target="tpu_custom_call" | custom-call | flops 1811939328 | bytes 7471104 | tf_op jit(solution)/shard_map/output/pallas_call | solution.py:148
  214.3 9.7 %all-to-all-start.1 = ((bf16[64,8,1024]{2,1,0:T(8,128)(2,1)}), bf16[64,8,1024]{2,1,0:T(8,128)(2,1)S(1)}, u32[]{:S(2)}, u32[]{:S(2)}) async-start(bf16[64,8,1024]{2,1,0:T(8,128)(2,1)} %bitcast.39), calls=%async_computation.1 | async-start | bytes 2097152 | tf_op jit(solution)/shard_map/all_to_all | solution.py:239
  224.8 1.5 moments.1
  226.4 11.7 %cholesky.16 = f32[128,128]{1,0:T(8,128)S(1)} custom-call(f32[128,128]{1,0:T(8,128)S(1)} %fusion.2), custom_call_target="Cholesky" | custom-call | tf_op jit(solution)/shard_map/jit(cholesky)/cholesky | solution.py:254
  239.5 9.8 %custom-call.7 = f32[1,128,128]{1,2,0:T(8,128)S(1)} custom-call(f32[1,128,128]{2,1,0:T(8,128)S(1)} %fusion), custom_call_target="InvertDiagBlocksLowerTriangular" | custom-call | tf_op jit(solution)/shard_map/jit(_solve_triangular)/triangular_solve | solution.py:255
  249.3 1.0 convolution_bitcast_fusion
  250.3 2.3 all-to-all-done.1
  252.6 1.0 copy-done.6
  253.6 3.5 %combine.1 = bf16[128,1024]{1,0:T(8,128)(2,1)} custom-call(s32[128,4]{1,0:T(8,128)} %copy.10.routes_ref, f32[128,4]{1,0:T(8,128)} %copy.11.weights_ref, bf16[512,1024]{1,0:T(8,128)(2,1)} %bitcast.37, bf16[512,1024]{1,0:T(8,128)(2,1)} %bitcast.14.refs_1_), custom_call_target="tpu_custom_call" | custom-call | tf_op jit(solution)/shard_map/combine/pallas_call | solution.py:82
  (34 shorter events, 4.2 us)
Async XLA Ops:
  47.0 26.0 %collective-permute-start.10 = (bf16[512,1024]{1,0:T(8,128)(2,1)S(1)}, bf16[512,1024]{1,0:T(8,128)(2,1)}, u32[]{:S(2)}, u32[]{:S(2)}) collective-permute-start(bf16[512,1024]{1,0:T(8,128)(2,1)S(1)} %bitcast.34), channel_id=1, source_target_pairs={{0,64},{64,128},{128,192},{192,0},{1,65},{65,129},{129,193},{193,1... | collective-permute-start | bytes 3145736 | tf_op jit(solution)/shard_map/ppermute | solution.py:210
  48.2 26.0 %collective-permute-start.11 = (bf16[512,1024]{1,0:T(8,128)(2,1)S(1)}, bf16[512,1024]{1,0:T(8,128)(2,1)}, u32[]{:S(2)}, u32[]{:S(2)}) collective-permute-start(bf16[512,1024]{1,0:T(8,128)(2,1)S(1)} %bitcast.35), channel_id=1, source_target_pairs={{0,192},{64,0},{128,64},{192,128},{1,193},{65,1},{129,65},{193,129... | collective-permute-start | bytes 3145736 | tf_op jit(solution)/shard_map/ppermute | solution.py:210
  49.7 66.9 %all-to-all-start = ((bf16[64,8,1024]{2,1,0:T(8,128)(2,1)}), bf16[64,8,1024]{2,1,0:T(8,128)(2,1)S(1)}, u32[]{:S(2)}, u32[]{:S(2)}) async-start(bf16[64,8,1024]{2,1,0:T(8,128)(2,1)} %bitcast.1), calls=%async_computation | async-start | bytes 2097152 | tf_op jit(solution)/shard_map/all_to_all | solution.py:239
  56.5 2.2 copy-start.7
  60.0 53.6 %collective-permute-start = (bf16[384,1152]{1,0:T(8,128)(2,1)S(1)}, bf16[384,1152]{1,0:T(8,128)(2,1)S(1)}, u32[]{:S(2)}, u32[]{:S(2)}) collective-permute-start(bf16[384,1152]{1,0:T(8,128)(2,1)S(1)} %get-tuple-element.31), channel_id=1, source_target_pairs={{0,64},{64,128},{128,192},{192,0},{1,65},{65,129},{129,193},{193,1... | collective-permute-start | bytes 2654216 | tf_op jit(solution)/shard_map/ppermute | solution.py:210
  74.1 29.0 %collective-permute-start.12 = (bf16[256,1024]{1,0:T(8,128)(2,1)S(1)}, bf16[256,1024]{1,0:T(8,128)(2,1)S(1)}, u32[]{:S(2)}, u32[]{:S(2)}) collective-permute-start(bf16[256,1024]{1,0:T(8,128)(2,1)S(1)} %slice.30), channel_id=1, source_target_pairs={{0,64},{64,128},{128,192},{192,0},{1,65},{65,129},{129,193},{193,1... | collective-permute-start | bytes 1572872 | tf_op jit(solution)/shard_map/ppermute | solution.py:210
  75.3 27.8 %collective-permute-start.13 = (bf16[256,1024]{1,0:T(8,128)(2,1)S(1)}, bf16[256,1024]{1,0:T(8,128)(2,1)S(1)}, u32[]{:S(2)}, u32[]{:S(2)}) collective-permute-start(bf16[256,1024]{1,0:T(8,128)(2,1)S(1)} %slice.31), channel_id=1, source_target_pairs={{0,192},{64,0},{128,64},{192,128},{1,193},{65,1},{129,65},{193,129... | collective-permute-start | bytes 1572872 | tf_op jit(solution)/shard_map/ppermute | solution.py:210
  78.0 37.7 %collective-permute-start.1 = (bf16[384,1152]{1,0:T(8,128)(2,1)S(1)}, bf16[384,1152]{1,0:T(8,128)(2,1)S(1)}, u32[]{:S(2)}, u32[]{:S(2)}) collective-permute-start(bf16[384,1152]{1,0:T(8,128)(2,1)S(1)} %get-tuple-element.29), channel_id=1, source_target_pairs={{0,192},{64,0},{128,64},{192,128},{1,193},{65,1},{129,65},{193,129... | collective-permute-start | bytes 2654216 | tf_op jit(solution)/shard_map/ppermute | solution.py:210
  78.1 45.1 %collective-permute-start.9 = (bf16[384,1152]{1,0:T(8,128)(2,1)}, bf16[384,1152]{1,0:T(8,128)(2,1)}, u32[]{:S(2)}, u32[]{:S(2)}) collective-permute-start(bf16[384,1152]{1,0:T(8,128)(2,1)} %get-tuple-element.28), channel_id=1, source_target_pairs={{0,128},{64,192},{128,0},{192,64},{1,129},{65,193},{129,1},{193,65... | collective-permute-start | bytes 2654216 | tf_op jit(solution)/shard_map/ppermute | solution.py:210
  111.1 21.1 %collective-permute-start.14 = (bf16[512,384]{1,0:T(8,128)(2,1)S(1)}, bf16[512,384]{1,0:T(8,128)(2,1)S(1)}, u32[]{:S(2)}, u32[]{:S(2)}) collective-permute-start(bf16[512,384]{1,0:T(8,128)(2,1)S(1)} %hidden.3.refs_0_.refs_3_), channel_id=1, source_target_pairs={{0,64},{64,128},{128,192},{192,0},{1,65},{65,129},{129,193},{193,1... | collective-permute-start | bytes 1179656 | tf_op jit(solution)/shard_map/ppermute | solution.py:210
  111.2 28.9 %collective-permute-start.15 = (bf16[512,384]{1,0:T(8,128)(2,1)S(1)}, bf16[512,384]{1,0:T(8,128)(2,1)S(1)}, u32[]{:S(2)}, u32[]{:S(2)}) collective-permute-start(bf16[512,384]{1,0:T(8,128)(2,1)S(1)} %hidden.3.refs_0_.refs_3_), channel_id=1, source_target_pairs={{0,128},{64,192},{128,0},{192,64},{1,129},{65,193},{129,1},{193,65... | collective-permute-start | bytes 1179656 | tf_op jit(solution)/shard_map/ppermute | solution.py:210
  113.6 0.9 copy-start
  114.5 28.7 %collective-permute-start.16 = (bf16[512,384]{1,0:T(8,128)(2,1)S(1)}, bf16[512,384]{1,0:T(8,128)(2,1)}, u32[]{:S(2)}, u32[]{:S(2)}) collective-permute-start(bf16[512,384]{1,0:T(8,128)(2,1)S(1)} %hidden.3.refs_0_.refs_3_), channel_id=1, source_target_pairs={{0,192},{64,0},{128,64},{192,128},{1,193},{65,1},{129,65},{193,129... | collective-permute-start | bytes 1179656 | tf_op jit(solution)/shard_map/ppermute | solution.py:210
  115.7 0.9 copy-start.3
  116.6 43.9 %collective-permute-start.2 = (bf16[512,1024]{1,0:T(8,128)(2,1)S(1)}, bf16[512,1024]{1,0:T(8,128)(2,1)}, u32[]{:S(2)}, u32[]{:S(2)}) collective-permute-start(bf16[512,1024]{1,0:T(8,128)(2,1)S(1)} %bitcast.31), channel_id=1, source_target_pairs={{0,64},{64,128},{128,192},{192,0},{1,65},{65,129},{129,193},{193,1... | collective-permute-start | bytes 3145736 | tf_op jit(solution)/shard_map/ppermute | solution.py:210
  123.2 42.5 %collective-permute-start.3 = (bf16[512,1024]{1,0:T(8,128)(2,1)S(1)}, bf16[512,1024]{1,0:T(8,128)(2,1)}, u32[]{:S(2)}, u32[]{:S(2)}) collective-permute-start(bf16[512,1024]{1,0:T(8,128)(2,1)S(1)} %bitcast.32), channel_id=1, source_target_pairs={{0,192},{64,0},{128,64},{192,128},{1,193},{65,1},{129,65},{193,129... | collective-permute-start | bytes 3145736 | tf_op jit(solution)/shard_map/ppermute | solution.py:210
  143.2 1.2 copy-start.1
  144.4 1.2 copy-start.4
  150.5 63.8 %all-to-all-start.3 = ((bf16[64,8,1024]{2,1,0:T(8,128)(2,1)}), bf16[64,8,1024]{2,1,0:T(8,128)(2,1)}, u32[]{:S(2)}, u32[]{:S(2)}) async-start(bf16[64,8,1024]{2,1,0:T(8,128)(2,1)} %bitcast.38), calls=%async_computation.3 | async-start | bytes 2097152 | tf_op jit(solution)/shard_map/all_to_all | solution.py:239
  161.6 12.0 %collective-permute-start.4 = (bf16[256,1024]{1,0:T(8,128)(2,1)S(1)}, bf16[256,1024]{1,0:T(8,128)(2,1)S(1)}, u32[]{:S(2)}, u32[]{:S(2)}) collective-permute-start(bf16[256,1024]{1,0:T(8,128)(2,1)S(1)} %slice.28), channel_id=1, source_target_pairs={{0,64},{64,128},{128,192},{192,0},{1,65},{65,129},{129,193},{193,1... | collective-permute-start | bytes 1572872 | tf_op jit(solution)/shard_map/ppermute | solution.py:210
  166.8 42.7 %copy-start.2 = (bf16[384,1152]{1,0:T(8,128)(2,1)S(1)}, bf16[384,1152]{1,0:T(8,128)(2,1)}, u32[]{:S(2)}) copy-start(bf16[384,1152]{1,0:T(8,128)(2,1)} %copy-done) | copy-start | bytes 2654212
  166.8 42.7 %copy-start.5 = (bf16[384,1152]{1,0:T(8,128)(2,1)S(1)}, bf16[384,1152]{1,0:T(8,128)(2,1)}, u32[]{:S(2)}) copy-start(bf16[384,1152]{1,0:T(8,128)(2,1)} %copy-done.3) | copy-start | bytes 2654212
  166.8 14.4 %collective-permute-start.5 = (bf16[256,1024]{1,0:T(8,128)(2,1)S(1)}, bf16[256,1024]{1,0:T(8,128)(2,1)S(1)}, u32[]{:S(2)}, u32[]{:S(2)}) collective-permute-start(bf16[256,1024]{1,0:T(8,128)(2,1)S(1)} %slice.29), channel_id=1, source_target_pairs={{0,192},{64,0},{128,64},{192,128},{1,193},{65,1},{129,65},{193,129... | collective-permute-start | bytes 1572872 | tf_op jit(solution)/shard_map/ppermute | solution.py:210
  189.2 10.2 %collective-permute-start.6 = (bf16[512,384]{1,0:T(8,128)(2,1)S(1)}, bf16[512,384]{1,0:T(8,128)(2,1)S(1)}, u32[]{:S(2)}, u32[]{:S(2)}) collective-permute-start(bf16[512,384]{1,0:T(8,128)(2,1)S(1)} %hidden.2.refs_0_.refs_2_), channel_id=1, source_target_pairs={{0,64},{64,128},{128,192},{192,0},{1,65},{65,129},{129,193},{193,1... | collective-permute-start | bytes 1179656 | tf_op jit(solution)/shard_map/ppermute | solution.py:210
  190.7 17.0 %collective-permute-start.7 = (bf16[512,384]{1,0:T(8,128)(2,1)S(1)}, bf16[512,384]{1,0:T(8,128)(2,1)S(1)}, u32[]{:S(2)}, u32[]{:S(2)}) collective-permute-start(bf16[512,384]{1,0:T(8,128)(2,1)S(1)} %hidden.2.refs_0_.refs_2_), channel_id=1, source_target_pairs={{0,128},{64,192},{128,0},{192,64},{1,129},{65,193},{129,1},{193,65... | collective-permute-start | bytes 1179656 | tf_op jit(solution)/shard_map/ppermute | solution.py:210
  192.6 16.9 %collective-permute-start.8 = (bf16[512,384]{1,0:T(8,128)(2,1)S(1)}, bf16[512,384]{1,0:T(8,128)(2,1)S(1)}, u32[]{:S(2)}, u32[]{:S(2)}) collective-permute-start(bf16[512,384]{1,0:T(8,128)(2,1)S(1)} %hidden.2.refs_0_.refs_2_), channel_id=1, source_target_pairs={{0,192},{64,0},{128,64},{192,128},{1,193},{65,1},{129,65},{193,129... | collective-permute-start | bytes 1179656 | tf_op jit(solution)/shard_map/ppermute | solution.py:210
  214.3 9.7 %copy-start.8 = (f32[128,4]{0,1:T(4,128)S(1)}, f32[128,4]{0,1:T(4,128)}, u32[]{:S(2)}) copy-start(f32[128,4]{0,1:T(4,128)} %param.9) | copy-start | bytes 6148
  214.3 38.3 %all-to-all-start.1 = ((bf16[64,8,1024]{2,1,0:T(8,128)(2,1)}), bf16[64,8,1024]{2,1,0:T(8,128)(2,1)S(1)}, u32[]{:S(2)}, u32[]{:S(2)}) async-start(bf16[64,8,1024]{2,1,0:T(8,128)(2,1)} %bitcast.39), calls=%async_computation.1 | async-start | bytes 2097152 | tf_op jit(solution)/shard_map/all_to_all | solution.py:239
  252.6 1.0 copy-start.6

commit v3 on v2

--- a/solution.py
+++ b/solution.py
@@ -210,6 +210,22 @@
     return lax.ppermute(value, "dp", [(i, (i + shift) % splits) for i in range(splits)])
 
 
+def after_kernel(*refs):
+    pass
+
+
+def after(value, *others):
+    anywhere = pl.BlockSpec(memory_space=pl.ANY)
+    return pl.pallas_call(
+        after_kernel,
+        out_shape=jax.ShapeDtypeStruct(value.shape, value.dtype),
+        in_specs=[anywhere] * (1 + len(others)),
+        out_specs=anywhere,
+        input_output_aliases={0: 0},
+        name="after",
+    )(value, *others)
+
+
 def turn_down(down_weight, basis, width):
     splits, me = lax.axis_size("dp"), lax.axis_index("dp")
     pieces = []
@@ -241,9 +257,9 @@
     down = turn_down(down_weight[0], sketch_basis, width)
     own, sketch_rows, returned = [], [], []
     for outgoing in dispatch(routes, tokens, experts, CUTS):
-        arrived = swap(outgoing)
+        arrived = swap(outgoing if not own else after(outgoing, arrived))
         if not own:
-            arrived, down[1], down[3] = lax.optimization_barrier((arrived, down[1], down[3]))
+            arrived = after(arrived, down[1], down[3])
         hidden = hidden_of(me, around(arrived), gate_weight[0], up_weight[0])
         everywhere = [hidden] + [shift_by(hidden, s) for s in range(1, lax.axis_size("dp"))]
         out, rows = output_of(everywhere, down, width)

time: 258 us -> 250 us (0.969)
  blocking collectives: 41.7 us -> 0 us
  starting transfers between devices: 48.9 us -> 89.8 us
  waiting for transfers between devices: 92.6 us -> 87.7 us
  local copies, waits for them, and re-layouts: 13.9 us -> 10.9 us
    all_to_all x1 -> x0, blocking collectives: 41.7 us -> none  [swap(): lax.all_to_all(blocks, 'expert', split_axis=0, concat_axis=0, tiled=True)]
    all_to_all x3 -> x4, starting transfers between devices: 26.4 us -> 64.8 us  [swap(): lax.all_to_all(blocks, 'expert', split_axis=0, concat_axis=0, tiled=True)]
    ppermute x17, waiting for transfers between devices: 90.3 us -> 82.5 us  [shift_by(): lax.ppermute(value, 'dp', [(i, (i + shift) % splits) for i in range(split...]
    unnamed x20 -> x16, local copies, waits for them, and re-layouts: 7.33 us -> 4.31 us
    all_to_all x3 -> x4, waiting for transfers between devices: 2.28 us -> 5.18 us  [swap(): lax.all_to_all(blocks, 'expert', split_axis=0, concat_axis=0, tiled=True)]
  transfers between devices with their start and end apart: 20 -> 21, of which waited for: 13 -> 13; matrix products, arithmetic and copies ran while one was open for 13% -> 13% of each run, Pallas kernels for 11% -> 11%
where the time goes in v3:
time: 250 us; the launch traced here: 249 us
  starting transfers between devices  89.8 us (36%)
  waiting for transfers between devices  87.7 us (35%)
  Pallas kernels  34.4 us (14%)
  other arithmetic  24.2 us (10%)
  local copies, waits for them, and re-layouts  10.9 us (4%)
    ppermute x17, waiting for transfers between devices, shift_by(): lax.ppermute(value, 'dp', [(i, (i + shift) % splits) for i in range(split...  82.5 us
    all_to_all x4, starting transfers between devices, swap(): lax.all_to_all(blocks, 'expert', split_axis=0, concat_axis=0, tiled=True)  64.8 us
    ppermute x17, starting transfers between devices, shift_by(): lax.ppermute(value, 'dp', [(i, (i + shift) % splits) for i in range(split...  25 us
    pallas_call x2, Pallas kernels, hidden_of(): pl.pallas_call(hidden_kernel, grid_spec=pltpu.PrefetchScalarGridSpec(num_...  15.8 us
    another operation x3, other arithmetic, body(): lower_factor = jnp.linalg.cholesky(gram)  12.4 us
    another operation x2, other arithmetic, body(): jax.scipy.linalg.solve_triangular(lower_factor, projected, lower=True)  10.5 us
    pallas_call x2, Pallas kernels, output_of(): pl.pallas_call(functools.partial(output_kernel, parts), grid=(count // bl...  10.3 us
    all_to_all x4, waiting for transfers between devices, swap(): lax.all_to_all(blocks, 'expert', split_axis=0, concat_axis=0, tiled=True)  5.18 us
  transfers between devices with their start and end apart: 21, of which 13 were waited for; matrix products, arithmetic and copies ran while one was open for 13% of the time, Pallas kernels for 11%

profile of v3, /device:TPU:1, one launch (start us, length us, event | category | flops | bytes accessed | tf_op | source)
XLA Modules:
  0.0 248.9 jit_solution(5574595595388813093)
XLA Ops:
  0.6 1.4 copy.12.routes_ref
  2.0 3.2 %dispatch.1 = (bf16[512,1024]{1,0:T(8,128)(2,1)}, bf16[512,1024]{1,0:T(8,128)(2,1)}) custom-call(s32[128,4]{1,0:T(8,128)} %copy.12.routes_ref, bf16[128,1024]{1,0:T(8,128)(2,1)} %tokens_ref.1), custom_call_target="tpu_custom_call" | custom-call | tf_op jit(solution)/shard_map/dispatch/pallas_call | solution.py:52
  5.2 13.2 %all-to-all-start = ((bf16[64,8,1024]{2,1,0:T(8,128)(2,1)}), bf16[64,8,1024]{2,1,0:T(8,128)(2,1)S(1)}, u32[]{:S(2)}, u32[]{:S(2)}) async-start(bf16[64,8,1024]{2,1,0:T(8,128)(2,1)} %bitcast.36), calls=%async_computation | async-start | bytes 2097152 | tf_op jit(solution)/shard_map/all_to_all | solution.py:255
  18.4 2.2 dynamic-slice_bitcast_fusion
  20.7 1.3 pad_maximum_fusion
  22.0 1.2 collective-permute-start
  23.2 1.5 collective-permute-start.1
  24.7 19.3 %collective-permute-done.refs_1_.refs_5_ = bf16[384,1152]{1,0:T(8,128)(2,1)S(1)} collective-permute-done((bf16[384,1152]{1,0:T(8,128)(2,1)S(1)}, bf16[384,1152]{1,0:T(8,128)(2,1)S(1)}, u32[]{:S(2)}, u32[]{:S(2)}) %collective-permute-start) | collective-permute-done | bytes 884768 | tf_op jit(solution)/shard_map/ppermute | solution.py:210
  44.0 3.0 %all-to-all-done = bf16[64,8,1024]{2,1,0:T(8,128)(2,1)S(1)} async-done(((bf16[64,8,1024]{2,1,0:T(8,128)(2,1)}), bf16[64,8,1024]{2,1,0:T(8,128)(2,1)S(1)}, u32[]{:S(2)}, u32[]{:S(2)}) %all-to-all-start) | async-done | bytes 1048608 | tf_op jit(solution)/shard_map/all_to_all | solution.py:255
  47.0 1.0 copy-done
  47.9 1.2 collective-permute-start.2
  49.2 1.5 collective-permute-start.3
  50.6 9.2 %all-to-all-start.2 = ((bf16[64,8,1024]{2,1,0:T(8,128)(2,1)}), bf16[64,8,1024]{2,1,0:T(8,128)(2,1)S(1)}, u32[]{:S(2)}, u32[]{:S(2)}) async-start(bf16[64,8,1024]{2,1,0:T(8,128)(2,1)} %bitcast.35), calls=%async_computation.2 | async-start | bytes 2097152 | tf_op jit(solution)/shard_map/all_to_all | solution.py:255
  59.9 14.3 %collective-permute-done.2.left_ref = bf16[512,1024]{1,0:T(8,128)(2,1)} collective-permute-done((bf16[512,1024]{1,0:T(8,128)(2,1)}, bf16[512,1024]{1,0:T(8,128)(2,1)}, u32[]{:S(2)}, u32[]{:S(2)}) %collective-permute-start.2) | collective-permute-done | bytes 1048608 | tf_op jit(solution)/shard_map/ppermute | solution.py:210
  74.2 1.1 slice.28
  75.4 1.1 slice.29
  76.5 2.7 %collective-permute-start.5 = (bf16[256,1024]{1,0:T(8,128)(2,1)S(1)}, bf16[256,1024]{1,0:T(8,128)(2,1)S(1)}, u32[]{:S(2)}, u32[]{:S(2)}) collective-permute-start(bf16[256,1024]{1,0:T(8,128)(2,1)S(1)} %slice.29), channel_id=1, source_target_pairs={{0,192},{64,0},{128,64},{192,128},{1,193},{65,1},{129,65},{193,129... | collective-permute-start | bytes 1572872 | tf_op jit(solution)/shard_map/ppermute | solution.py:210
  79.5 9.8 %collective-permute-done.4.top_ref = bf16[256,1024]{1,0:T(8,128)(2,1)S(1)} collective-permute-done((bf16[256,1024]{1,0:T(8,128)(2,1)S(1)}, bf16[256,1024]{1,0:T(8,128)(2,1)S(1)}, u32[]{:S(2)}, u32[]{:S(2)}) %collective-permute-start.4) | collective-permute-done | bytes 524320 | tf_op jit(solution)/shard_map/ppermute | solution.py:210
  89.4 0.9 collective-permute-done.5.bottom_ref
  90.2 7.9 %hidden.2.refs_0_.refs_2_ = bf16[512,384]{1,0:T(8,128)(2,1)S(1)} custom-call(s32[1]{0:T(128)} %bitcast.me_ref, bf16[512,1024]{1,0:T(8,128)(2,1)S(1)} %copy-done.1, bf16[512,1024]{1,0:T(8,128)(2,1)} %collective-permute-done.2.left_ref, bf16[512,1024]{1,0:T(8,128)(2,1)} %collective-permute-done.3.right_ref, ...), custom_call_target="tpu_custom_call" | custom-call | flops 3221225472 | bytes 10878976 | tf_op jit(solution)/shard_map/hidden/pallas_call | solution.py:114
  98.2 5.1 %collective-permute-start.7 = (bf16[512,384]{1,0:T(8,128)(2,1)S(1)}, bf16[512,384]{1,0:T(8,128)(2,1)S(1)}, u32[]{:S(2)}, u32[]{:S(2)}) collective-permute-start(bf16[512,384]{1,0:T(8,128)(2,1)S(1)} %hidden.2.refs_0_.refs_2_), channel_id=1, source_target_pairs={{0,128},{64,192},{128,0},{192,64},{1,129},{65,193},{129,1},{193,65... | collective-permute-start | bytes 1179656 | tf_op jit(solution)/shard_map/ppermute | solution.py:210
  103.3 1.5 collective-permute-start.10
  104.8 3.2 %collective-permute-done.9.refs_6_ = bf16[384,1152]{1,0:T(8,128)(2,1)} collective-permute-done((bf16[384,1152]{1,0:T(8,128)(2,1)}, bf16[384,1152]{1,0:T(8,128)(2,1)}, u32[]{:S(2)}, u32[]{:S(2)}) %collective-permute-start.9) | collective-permute-done | bytes 884768 | tf_op jit(solution)/shard_map/ppermute | solution.py:210
  108.0 2.3 collective-permute-start.11
  110.3 7.3 %collective-permute-done.6.refs_1_ = bf16[512,384]{1,0:T(8,128)(2,1)S(1)} collective-permute-done((bf16[512,384]{1,0:T(8,128)(2,1)S(1)}, bf16[512,384]{1,0:T(8,128)(2,1)S(1)}, u32[]{:S(2)}, u32[]{:S(2)}) %collective-permute-start.6) | collective-permute-done | bytes 393248 | tf_op jit(solution)/shard_map/ppermute | solution.py:210
  117.6 0.7 collective-permute-done.8.refs_3_
  118.3 1.2 copy-done.3
  119.5 5.2 %output.2 = (bf16[512,1024]{1,0:T(8,128)(2,1)}, f32[512,128]{1,0:T(8,128)S(1)}) custom-call(bf16[512,384]{1,0:T(8,128)(2,1)S(1)} %hidden.2.refs_0_.refs_2_, bf16[512,384]{1,0:T(8,128)(2,1)S(1)} %collective-permute-done.6.refs_1_, bf16[512,384]{1,0:T(8,128)(2,1)S(1)} %collective-permute-done.7.refs_2_, bf16[512,384]{1,0:T(8,128)(2,1)} %collective-permute-done.8.refs_3_, ...), custom_call_target="tpu_custom_call" | custom-call | flops 1811939328 | bytes 7471104 | tf_op jit(solution)/shard_map/output/pallas_call | solution.py:148
  124.7 28.3 %all-to-all-start.1 = ((bf16[64,8,1024]{2,1,0:T(8,128)(2,1)}), bf16[64,8,1024]{2,1,0:T(8,128)(2,1)}, u32[]{:S(2)}, u32[]{:S(2)}) async-start(bf16[64,8,1024]{2,1,0:T(8,128)(2,1)} %bitcast.37), calls=%async_computation.1 | async-start | bytes 2097152 | tf_op jit(solution)/shard_map/all_to_all | solution.py:255
  153.1 1.1 slice.30
  154.2 1.1 slice.31
  155.3 2.7 %collective-permute-start.13 = (bf16[256,1024]{1,0:T(8,128)(2,1)S(1)}, bf16[256,1024]{1,0:T(8,128)(2,1)S(1)}, u32[]{:S(2)}, u32[]{:S(2)}) collective-permute-start(bf16[256,1024]{1,0:T(8,128)(2,1)S(1)} %slice.31), channel_id=1, source_target_pairs={{0,192},{64,0},{128,64},{192,128},{1,193},{65,1},{129,65},{193,129... | collective-permute-start | bytes 1572872 | tf_op jit(solution)/shard_map/ppermute | solution.py:210
  158.1 10.4 %collective-permute-done.12.top_ref = bf16[256,1024]{1,0:T(8,128)(2,1)S(1)} collective-permute-done((bf16[256,1024]{1,0:T(8,128)(2,1)S(1)}, bf16[256,1024]{1,0:T(8,128)(2,1)S(1)}, u32[]{:S(2)}, u32[]{:S(2)}) %collective-permute-start.12) | collective-permute-done | bytes 524320 | tf_op jit(solution)/shard_map/ppermute | solution.py:210
  168.5 7.9 %hidden.3.refs_0_.refs_3_ = bf16[512,384]{1,0:T(8,128)(2,1)S(1)} custom-call(s32[1]{0:T(128)} %bitcast.me_ref, bf16[512,1024]{1,0:T(8,128)(2,1)S(1)} %bitcast.34, bf16[512,1024]{1,0:T(8,128)(2,1)} %collective-permute-done.10.left_ref, bf16[512,1024]{1,0:T(8,128)(2,1)} %collective-permute-done.11.right_ref, ...), custom_call_target="tpu_custom_call" | custom-call | flops 3221225472 | bytes 10878976 | tf_op jit(solution)/shard_map/hidden/pallas_call | solution.py:114
  176.4 1.0 collective-permute-start.14
  177.4 3.8 %collective-permute-start.15 = (bf16[512,384]{1,0:T(8,128)(2,1)S(1)}, bf16[512,384]{1,0:T(8,128)(2,1)S(1)}, u32[]{:S(2)}, u32[]{:S(2)}) collective-permute-start(bf16[512,384]{1,0:T(8,128)(2,1)S(1)} %hidden.3.refs_0_.refs_3_), channel_id=1, source_target_pairs={{0,128},{64,192},{128,0},{192,64},{1,129},{65,193},{129,1},{193,65... | collective-permute-start | bytes 1179656 | tf_op jit(solution)/shard_map/ppermute | solution.py:210
  181.2 6.6 %collective-permute-done.14.refs_1_ = bf16[512,384]{1,0:T(8,128)(2,1)S(1)} collective-permute-done((bf16[512,384]{1,0:T(8,128)(2,1)S(1)}, bf16[512,384]{1,0:T(8,128)(2,1)S(1)}, u32[]{:S(2)}, u32[]{:S(2)}) %collective-permute-start.14) | collective-permute-done | bytes 393248 | tf_op jit(solution)/shard_map/ppermute | solution.py:210
  187.9 9.3 %collective-permute-done.15.refs_2_ = bf16[512,384]{1,0:T(8,128)(2,1)S(1)} collective-permute-done((bf16[512,384]{1,0:T(8,128)(2,1)S(1)}, bf16[512,384]{1,0:T(8,128)(2,1)S(1)}, u32[]{:S(2)}, u32[]{:S(2)}) %collective-permute-start.15) | collective-permute-done | bytes 393248 | tf_op jit(solution)/shard_map/ppermute | solution.py:210
  197.7 5.1 %output.3 = (bf16[512,1024]{1,0:T(8,128)(2,1)}, f32[512,128]{1,0:T(8,128)S(1)}) custom-call(bf16[512,384]{1,0:T(8,128)(2,1)S(1)} %hidden.3.refs_0_.refs_3_, bf16[512,384]{1,0:T(8,128)(2,1)S(1)} %collective-permute-done.14.refs_1_, bf16[512,384]{1,0:T(8,128)(2,1)S(1)} %collective-permute-done.15.refs_2_, ...), custom_call_target="tpu_custom_call" | custom-call | flops 1811939328 | bytes 7471104 | tf_op jit(solution)/shard_map/output/pallas_call | solution.py:148
  202.8 14.1 %all-to-all-start.3 = ((bf16[64,8,1024]{2,1,0:T(8,128)(2,1)}), bf16[64,8,1024]{2,1,0:T(8,128)(2,1)}, u32[]{:S(2)}, u32[]{:S(2)}) async-start(bf16[64,8,1024]{2,1,0:T(8,128)(2,1)} %bitcast.38), calls=%async_computation.3 | async-start | bytes 2097152 | tf_op jit(solution)/shard_map/all_to_all | solution.py:255
  216.9 0.7 copy.13.weights_ref
  217.7 1.5 moments.1
  219.3 11.7 %cholesky.16 = f32[128,128]{1,0:T(8,128)S(1)} custom-call(f32[128,128]{1,0:T(8,128)S(1)} %fusion.2), custom_call_target="Cholesky" | custom-call | tf_op jit(solution)/shard_map/jit(cholesky)/cholesky | solution.py:270
  231.7 0.7 fusion
  232.4 9.8 %custom-call.7 = f32[1,128,128]{1,2,0:T(8,128)S(1)} custom-call(f32[1,128,128]{2,1,0:T(8,128)S(1)} %fusion), custom_call_target="InvertDiagBlocksLowerTriangular" | custom-call | tf_op jit(solution)/shard_map/jit(_solve_triangular)/triangular_solve | solution.py:271
  242.2 1.1 convolution_bitcast_fusion
  243.2 2.2 all-to-all-done.3
  245.4 3.5 %combine.1 = bf16[128,1024]{1,0:T(8,128)(2,1)} custom-call(s32[128,4]{1,0:T(8,128)} %copy.12.routes_ref, f32[128,4]{1,0:T(8,128)} %copy.13.weights_ref, bf16[512,1024]{1,0:T(8,128)(2,1)} %bitcast.10.refs_0_, bf16[512,1024]{1,0:T(8,128)(2,1)} %bitcast.14.refs_1_), custom_call_target="tpu_custom_call" | custom-call | tf_op jit(solution)/shard_map/combine/pallas_call | solution.py:82
  (33 shorter events, 1.9 us)
Async XLA Ops:
  5.2 41.7 %all-to-all-start = ((bf16[64,8,1024]{2,1,0:T(8,128)(2,1)}), bf16[64,8,1024]{2,1,0:T(8,128)(2,1)S(1)}, u32[]{:S(2)}, u32[]{:S(2)}) async-start(bf16[64,8,1024]{2,1,0:T(8,128)(2,1)} %bitcast.36), calls=%async_computation | async-start | bytes 2097152 | tf_op jit(solution)/shard_map/all_to_all | solution.py:255
  18.4 2.2 copy-start.5
  22.0 22.0 %collective-permute-start = (bf16[384,1152]{1,0:T(8,128)(2,1)S(1)}, bf16[384,1152]{1,0:T(8,128)(2,1)S(1)}, u32[]{:S(2)}, u32[]{:S(2)}) collective-permute-start(bf16[384,1152]{1,0:T(8,128)(2,1)S(1)} %get-tuple-element.25), channel_id=1, source_target_pairs={{0,64},{64,128},{128,192},{192,0},{1,65},{65,129},{129,193},{193,1... | collective-permute-start | bytes 2654216 | tf_op jit(solution)/shard_map/ppermute | solution.py:210
  23.2 20.8 %collective-permute-start.1 = (bf16[384,1152]{1,0:T(8,128)(2,1)S(1)}, bf16[384,1152]{1,0:T(8,128)(2,1)}, u32[]{:S(2)}, u32[]{:S(2)}) collective-permute-start(bf16[384,1152]{1,0:T(8,128)(2,1)S(1)} %get-tuple-element.23), channel_id=1, source_target_pairs={{0,192},{64,0},{128,64},{192,128},{1,193},{65,1},{129,65},{193,129... | collective-permute-start | bytes 2654216 | tf_op jit(solution)/shard_map/ppermute | solution.py:210
  44.0 3.0 %copy-start.2 = (bf16[384,1152]{1,0:T(8,128)(2,1)}, bf16[384,1152]{1,0:T(8,128)(2,1)S(1)}, u32[]{:S(2)}) copy-start(bf16[384,1152]{1,0:T(8,128)(2,1)S(1)} %collective-permute-done.refs_1_.refs_5_) | copy-start | bytes 2654212
  47.0 1.0 copy-start
  47.9 26.3 %collective-permute-start.2 = (bf16[512,1024]{1,0:T(8,128)(2,1)}, bf16[512,1024]{1,0:T(8,128)(2,1)}, u32[]{:S(2)}, u32[]{:S(2)}) collective-permute-start(bf16[512,1024]{1,0:T(8,128)(2,1)} %after.2.own_ref.refs_1_), channel_id=1, source_target_pairs={{0,64},{64,128},{128,192},{192,0},{1,65},{65,129},{129,193},{193,1... | collective-permute-start | bytes 3145736 | tf_op jit(solution)/shard_map/ppermute | solution.py:210
  49.2 26.2 %collective-permute-start.3 = (bf16[512,1024]{1,0:T(8,128)(2,1)}, bf16[512,1024]{1,0:T(8,128)(2,1)}, u32[]{:S(2)}, u32[]{:S(2)}) collective-permute-start(bf16[512,1024]{1,0:T(8,128)(2,1)} %after.2.own_ref.refs_1_), channel_id=1, source_target_pairs={{0,192},{64,0},{128,64},{192,128},{1,193},{65,1},{129,65},{193,129... | collective-permute-start | bytes 3145736 | tf_op jit(solution)/shard_map/ppermute | solution.py:210
  50.6 39.6 %copy-start.1 = (bf16[512,1024]{1,0:T(8,128)(2,1)S(1)}, bf16[512,1024]{1,0:T(8,128)(2,1)}, u32[]{:S(2)}) copy-start(bf16[512,1024]{1,0:T(8,128)(2,1)} %after.2.own_ref.refs_1_) | copy-start | bytes 3145732
  50.6 52.7 %all-to-all-start.2 = ((bf16[64,8,1024]{2,1,0:T(8,128)(2,1)}), bf16[64,8,1024]{2,1,0:T(8,128)(2,1)S(1)}, u32[]{:S(2)}, u32[]{:S(2)}) async-start(bf16[64,8,1024]{2,1,0:T(8,128)(2,1)} %bitcast.35), calls=%async_computation.2 | async-start | bytes 2097152 | tf_op jit(solution)/shard_map/all_to_all | solution.py:255
  75.3 14.1 %collective-permute-start.4 = (bf16[256,1024]{1,0:T(8,128)(2,1)S(1)}, bf16[256,1024]{1,0:T(8,128)(2,1)S(1)}, u32[]{:S(2)}, u32[]{:S(2)}) collective-permute-start(bf16[256,1024]{1,0:T(8,128)(2,1)S(1)} %slice.28), channel_id=1, source_target_pairs={{0,64},{64,128},{128,192},{192,0},{1,65},{65,129},{129,193},{193,1... | collective-permute-start | bytes 1572872 | tf_op jit(solution)/shard_map/ppermute | solution.py:210
  76.5 13.8 %collective-permute-start.5 = (bf16[256,1024]{1,0:T(8,128)(2,1)S(1)}, bf16[256,1024]{1,0:T(8,128)(2,1)S(1)}, u32[]{:S(2)}, u32[]{:S(2)}) collective-permute-start(bf16[256,1024]{1,0:T(8,128)(2,1)S(1)} %slice.29), channel_id=1, source_target_pairs={{0,192},{64,0},{128,64},{192,128},{1,193},{65,1},{129,65},{193,129... | collective-permute-start | bytes 1572872 | tf_op jit(solution)/shard_map/ppermute | solution.py:210
  79.2 28.8 %collective-permute-start.9 = (bf16[384,1152]{1,0:T(8,128)(2,1)}, bf16[384,1152]{1,0:T(8,128)(2,1)}, u32[]{:S(2)}, u32[]{:S(2)}) collective-permute-start(bf16[384,1152]{1,0:T(8,128)(2,1)} %get-tuple-element.22), channel_id=1, source_target_pairs={{0,128},{64,192},{128,0},{192,64},{1,129},{65,193},{129,1},{193,65... | collective-permute-start | bytes 2654216 | tf_op jit(solution)/shard_map/ppermute | solution.py:210
  98.1 19.4 %collective-permute-start.6 = (bf16[512,384]{1,0:T(8,128)(2,1)S(1)}, bf16[512,384]{1,0:T(8,128)(2,1)S(1)}, u32[]{:S(2)}, u32[]{:S(2)}) collective-permute-start(bf16[512,384]{1,0:T(8,128)(2,1)S(1)} %hidden.2.refs_0_.refs_2_), channel_id=1, source_target_pairs={{0,64},{64,128},{128,192},{192,0},{1,65},{65,129},{129,193},{193,1... | collective-permute-start | bytes 1179656 | tf_op jit(solution)/shard_map/ppermute | solution.py:210
  98.2 19.4 %collective-permute-start.7 = (bf16[512,384]{1,0:T(8,128)(2,1)S(1)}, bf16[512,384]{1,0:T(8,128)(2,1)S(1)}, u32[]{:S(2)}, u32[]{:S(2)}) collective-permute-start(bf16[512,384]{1,0:T(8,128)(2,1)S(1)} %hidden.2.refs_0_.refs_2_), channel_id=1, source_target_pairs={{0,128},{64,192},{128,0},{192,64},{1,129},{65,193},{129,1},{193,65... | collective-permute-start | bytes 1179656 | tf_op jit(solution)/shard_map/ppermute | solution.py:210
  103.3 15.0 %collective-permute-start.8 = (bf16[512,384]{1,0:T(8,128)(2,1)S(1)}, bf16[512,384]{1,0:T(8,128)(2,1)}, u32[]{:S(2)}, u32[]{:S(2)}) collective-permute-start(bf16[512,384]{1,0:T(8,128)(2,1)S(1)} %hidden.2.refs_0_.refs_2_), channel_id=1, source_target_pairs={{0,192},{64,0},{128,64},{192,128},{1,193},{65,1},{129,65},{193,129... | collective-permute-start | bytes 1179656 | tf_op jit(solution)/shard_map/ppermute | solution.py:210
  103.3 49.7 %collective-permute-start.10 = (bf16[512,1024]{1,0:T(8,128)(2,1)S(1)}, bf16[512,1024]{1,0:T(8,128)(2,1)}, u32[]{:S(2)}, u32[]{:S(2)}) collective-permute-start(bf16[512,1024]{1,0:T(8,128)(2,1)S(1)} %bitcast.32), channel_id=1, source_target_pairs={{0,64},{64,128},{128,192},{192,0},{1,65},{65,129},{129,193},{193,1... | collective-permute-start | bytes 3145736 | tf_op jit(solution)/shard_map/ppermute | solution.py:210
  108.0 46.2 %collective-permute-start.11 = (bf16[512,1024]{1,0:T(8,128)(2,1)S(1)}, bf16[512,1024]{1,0:T(8,128)(2,1)}, u32[]{:S(2)}, u32[]{:S(2)}) collective-permute-start(bf16[512,1024]{1,0:T(8,128)(2,1)S(1)} %bitcast.33), channel_id=1, source_target_pairs={{0,192},{64,0},{128,64},{192,128},{1,193},{65,1},{129,65},{193,129... | collective-permute-start | bytes 3145736 | tf_op jit(solution)/shard_map/ppermute | solution.py:210
  118.3 1.2 copy-start.3
  124.7 78.1 %all-to-all-start.1 = ((bf16[64,8,1024]{2,1,0:T(8,128)(2,1)}), bf16[64,8,1024]{2,1,0:T(8,128)(2,1)}, u32[]{:S(2)}, u32[]{:S(2)}) async-start(bf16[64,8,1024]{2,1,0:T(8,128)(2,1)} %bitcast.37), calls=%async_computation.1 | async-start | bytes 2097152 | tf_op jit(solution)/shard_map/all_to_all | solution.py:255
  154.1 14.3 %collective-permute-start.12 = (bf16[256,1024]{1,0:T(8,128)(2,1)S(1)}, bf16[256,1024]{1,0:T(8,128)(2,1)S(1)}, u32[]{:S(2)}, u32[]{:S(2)}) collective-permute-start(bf16[256,1024]{1,0:T(8,128)(2,1)S(1)} %slice.30), channel_id=1, source_target_pairs={{0,64},{64,128},{128,192},{192,0},{1,65},{65,129},{129,193},{193,1... | collective-permute-start | bytes 1572872 | tf_op jit(solution)/shard_map/ppermute | solution.py:210
  155.3 42.4 %copy-start.4 = (bf16[384,1152]{1,0:T(8,128)(2,1)S(1)}, bf16[384,1152]{1,0:T(8,128)(2,1)}, u32[]{:S(2)}) copy-start(bf16[384,1152]{1,0:T(8,128)(2,1)} %copy-done.2) | copy-start | bytes 2654212
  155.3 13.2 %collective-permute-start.13 = (bf16[256,1024]{1,0:T(8,128)(2,1)S(1)}, bf16[256,1024]{1,0:T(8,128)(2,1)S(1)}, u32[]{:S(2)}, u32[]{:S(2)}) collective-permute-start(bf16[256,1024]{1,0:T(8,128)(2,1)S(1)} %slice.31), channel_id=1, source_target_pairs={{0,192},{64,0},{128,64},{192,128},{1,193},{65,1},{129,65},{193,129... | collective-permute-start | bytes 1572872 | tf_op jit(solution)/shard_map/ppermute | solution.py:210
  176.4 11.4 %collective-permute-start.14 = (bf16[512,384]{1,0:T(8,128)(2,1)S(1)}, bf16[512,384]{1,0:T(8,128)(2,1)S(1)}, u32[]{:S(2)}, u32[]{:S(2)}) collective-permute-start(bf16[512,384]{1,0:T(8,128)(2,1)S(1)} %hidden.3.refs_0_.refs_3_), channel_id=1, source_target_pairs={{0,64},{64,128},{128,192},{192,0},{1,65},{65,129},{129,193},{193,1... | collective-permute-start | bytes 1179656 | tf_op jit(solution)/shard_map/ppermute | solution.py:210
  177.4 19.8 %collective-permute-start.15 = (bf16[512,384]{1,0:T(8,128)(2,1)S(1)}, bf16[512,384]{1,0:T(8,128)(2,1)S(1)}, u32[]{:S(2)}, u32[]{:S(2)}) collective-permute-start(bf16[512,384]{1,0:T(8,128)(2,1)S(1)} %hidden.3.refs_0_.refs_3_), channel_id=1, source_target_pairs={{0,128},{64,192},{128,0},{192,64},{1,129},{65,193},{129,1},{193,65... | collective-permute-start | bytes 1179656 | tf_op jit(solution)/shard_map/ppermute | solution.py:210
  181.2 16.5 %collective-permute-start.16 = (bf16[512,384]{1,0:T(8,128)(2,1)S(1)}, bf16[512,384]{1,0:T(8,128)(2,1)S(1)}, u32[]{:S(2)}, u32[]{:S(2)}) collective-permute-start(bf16[512,384]{1,0:T(8,128)(2,1)S(1)} %hidden.3.refs_0_.refs_3_), channel_id=1, source_target_pairs={{0,192},{64,0},{128,64},{192,128},{1,193},{65,1},{129,65},{193,129... | collective-permute-start | bytes 1179656 | tf_op jit(solution)/shard_map/ppermute | solution.py:210
  202.8 14.1 %copy-start.6 = (f32[128,4]{0,1:T(4,128)S(1)}, f32[128,4]{0,1:T(4,128)}, u32[]{:S(2)}) copy-start(f32[128,4]{0,1:T(4,128)} %param.9) | copy-start | bytes 6148
  202.8 42.6 %all-to-all-start.3 = ((bf16[64,8,1024]{2,1,0:T(8,128)(2,1)}), bf16[64,8,1024]{2,1,0:T(8,128)(2,1)}, u32[]{:S(2)}, u32[]{:S(2)}) async-start(bf16[64,8,1024]{2,1,0:T(8,128)(2,1)} %bitcast.38), calls=%async_computation.3 | async-start | bytes 2097152 | tf_op jit(solution)/shard_map/all_to_all | solution.py:255

commit v4 on v3

--- a/solution.py
+++ b/solution.py
@@ -10,7 +10,6 @@
 ridge_term = 1.0
 CUTS = (8, 8)
 VMEM = pl.BlockSpec(memory_space=pltpu.VMEM)
-
 
 def slot_codes(routes, experts):
     tokens, top = routes.shape
@@ -23,19 +22,16 @@
     before = jnp.dot(earlier, hit.astype(jnp.bfloat16), preferred_element_type=jnp.float32)
     return hits, jnp.where(hit > 0.0, before, -1.0)
 
-
 def spread(values, experts, slots):
     expert = lax.broadcasted_iota(jnp.int32, (experts, experts * slots), 0)
     at = lax.broadcasted_iota(jnp.int32, (experts, experts * slots), 1)
     ones = jnp.where(at // slots == expert, 1.0, 0.0).astype(jnp.bfloat16)
     return jnp.dot(values.astype(jnp.bfloat16), ones, preferred_element_type=jnp.float32)
 
-
 def in_slot(code, experts, slots, start):
     wide = spread(code, experts, slots)
     at = lax.broadcasted_iota(jnp.int32, wide.shape, 1)
     return wide == (lax.rem(at, slots) + start).astype(jnp.float32)
-
 
 def dispatch_kernel(experts, cuts, routes_ref, tokens_ref, *out_refs):
     _, code = slot_codes(routes_ref[...], experts)
@@ -46,7 +42,6 @@
         out_ref[...] = jnp.dot(chosen, tokens, preferred_element_type=jnp.float32).astype(out_ref.dtype)
         start += slots
 
-
 def dispatch(routes, tokens, experts, cuts):
     width = tokens.shape[1]
     return pl.pallas_call(
@@ -56,7 +51,6 @@
         out_specs=[VMEM] * len(cuts),
         name="dispatch",
     )(routes, tokens)
-
 
 def combine_kernel(experts, cuts, routes_ref, weights_ref, *refs):
     out_ref = refs[-1]
@@ -77,7 +71,6 @@
         start += slots
     out_ref[...] = total.astype(out_ref.dtype)
 
-
 def combine(routes, weights, rows, experts, cuts):
     return pl.pallas_call(
         functools.partial(combine_kernel, experts, cuts),
@@ -86,7 +79,6 @@
         out_specs=VMEM,
         name="combine",
     )(routes, weights, *rows)
-
 
 def hidden_kernel(me_ref, own_ref, left_ref, right_ref, top_ref, bottom_ref, gate_ref, up_ref, hidden_ref):
     width = own_ref.shape[1]
@@ -102,7 +94,6 @@
         up = up_term if up is None else up + up_term
     hidden_ref[...] = (gate / (1.0 + jnp.exp(-gate)) * up).astype(hidden_ref.dtype)
 
-
 def hidden_of(me, ring, gate_weight, up_weight):
     own, left, right, top, bottom = ring
     count, width = own.shape
@@ -128,7 +119,6 @@
         compiler_params=pltpu.CompilerParams(vmem_limit_bytes=48 << 20),
         name="hidden",
     )(me, own, left, right, top, bottom, gate_weight, up_weight)
-
 
 def output_kernel(parts, *refs):
     out_ref, sketch_ref = refs[-2:]
@@ -139,7 +129,6 @@
         total = term if total is None else total + term
     out_ref[...] = total[:, :width].astype(out_ref.dtype)
     sketch_ref[...] = total[:, width:]
-
 
 def output_of(hidden, down, width):
     count, units = hidden[0].shape
@@ -166,7 +155,6 @@
         compiler_params=pltpu.CompilerParams(vmem_limit_bytes=48 << 20),
         name="output",
     )(*hidden, *down)
-
 
 def moments_kernel(chunks, *refs):
     gram_ref, project_ref = refs[-2:]
@@ -189,7 +177,6 @@
     gram_ref[...] = gram + jnp.where(row == column, ridge_term, 0.0)
     project_ref[...] = project
 
-
 def moments(rows, own):
     size, units = rows[0].shape[1], own[0].shape[1]
     return pl.pallas_call(
@@ -204,15 +191,12 @@
         name="moments",
     )(*rows, *own)
 
-
 def shift_by(value, shift):
     splits = lax.axis_size("dp")
     return lax.ppermute(value, "dp", [(i, (i + shift) % splits) for i in range(splits)])
 
-
 def after_kernel(*refs):
     pass
-
 
 def after(value, *others):
     anywhere = pl.BlockSpec(memory_space=pl.ANY)
@@ -225,23 +209,25 @@
         name="after",
     )(value, *others)
 
-
 def turn_down(down_weight, basis, width):
     splits, me = lax.axis_size("dp"), lax.axis_index("dp")
-    pieces = []
-    for shift in range(splits):
-        to = lax.rem(me + shift, splits)
-        piece = lax.dynamic_slice_in_dim(down_weight, to * width, width, axis=1)
-        piece = jnp.concatenate([piece, basis], axis=1)
-        pieces.append(shift_by(piece, shift) if shift else piece)
-    return pieces
-
+    half = down_weight.shape[0] // 2
+
+    def piece(shift, rows):
+        at = lax.rem(me + shift, splits) * width
+        cut = lax.dynamic_slice(down_weight, (rows.start, at), (rows.stop - rows.start, width))
+        return jnp.concatenate([cut, basis[rows]], axis=1)
+
+    every, upper, lower = slice(0, 2 * half), slice(0, half), slice(half, 2 * half)
+    onward = shift_by(jnp.concatenate([piece(2, upper), piece(1, every)]), 1)
+    backward = shift_by(jnp.concatenate([piece(2, lower), piece(splits - 1, every)]), -1)
+    far = jnp.concatenate([shift_by(onward[:half], 1), shift_by(backward[:half], -1)])
+    return [piece(0, every), onward[half:], far, backward[half:]], (onward, backward)
 
 def around(own):
     half = own.shape[0] // 2
     left, right = shift_by(own, 1), shift_by(own, -1)
     return own, left, right, shift_by(left[:half], 1), shift_by(right[half:], -1)
-
 
 def body(tokens, routes, route_weights, gate_weight, up_weight, down_weight, sketch_basis):
     experts = lax.axis_size("expert")
@@ -254,24 +240,36 @@
         blocks = rows.reshape(experts, rows.shape[0] // experts, width)
         return lax.all_to_all(blocks, "expert", split_axis=0, concat_axis=0, tiled=True).reshape(rows.shape)
 
-    down = turn_down(down_weight[0], sketch_basis, width)
-    own, sketch_rows, returned = [], [], []
-    for outgoing in dispatch(routes, tokens, experts, CUTS):
-        arrived = swap(outgoing if not own else after(outgoing, arrived))
-        if not own:
-            arrived = after(arrived, down[1], down[3])
-        hidden = hidden_of(me, around(arrived), gate_weight[0], up_weight[0])
-        everywhere = [hidden] + [shift_by(hidden, s) for s in range(1, lax.axis_size("dp"))]
-        out, rows = output_of(everywhere, down, width)
-        own.append(hidden)
-        sketch_rows.append(rows)
-        returned.append(swap(out))
+    down, near = turn_down(down_weight[0], sketch_basis, width)
+    first, second = dispatch(routes, tokens, experts, CUTS)
+    gate, up = gate_weight[0], up_weight[0]
+
+    def spread_hidden(hidden):
+        return [hidden] + [shift_by(hidden, s) for s in range(1, lax.axis_size("dp"))]
+
+    rows0 = swap(first)
+    rows1 = swap(after(second, rows0))
+    rows0 = after(rows0, *near)
+    ring0 = around(rows0)
+    ring1 = around(rows1)
+    ring0 = (after(ring0[0], rows1),) + ring0[1:]
+    hidden0 = hidden_of(me, ring0, gate, up)
+
+    hidden1 = hidden_of(me, ring1, gate, up)
+    everywhere0 = spread_hidden(hidden0)
+
+    out0, sketch0 = output_of(everywhere0, down, width)
+    back0 = swap(out0)
+    everywhere1 = spread_hidden(hidden1)
+
+    out1, sketch1 = output_of(everywhere1, down, width)
+    back1 = swap(out1)
+    own, sketch_rows, returned = [hidden0, hidden1], [sketch0, sketch1], [back0, back1]
     gram, projected = moments(sketch_rows, own)
     lower_factor = jnp.linalg.cholesky(gram)
     whitened = jax.scipy.linalg.solve_triangular(lower_factor, projected, lower=True)
     mixed = combine(routes, route_weights, returned, experts, CUTS)
     return (mixed, whitened[None])
-
 
 def solution(mesh):
     return jax.shard_map(

time: 250 us -> 244 us (0.976)
  local copies, waits for them, and re-layouts: 10.9 us -> 29.5 us
  starting transfers between devices: 89.8 us -> 75 us
  waiting for transfers between devices: 87.7 us -> 80.7 us
  Pallas kernels: 34.4 us -> 31.4 us
    ppermute x17 -> x18, waiting for transfers between devices: 82.5 us -> 59.3 us  [shift_by(): lax.ppermute(value, 'dp', [(i, (i + shift) % splits) for i in range(split...]
    all_to_all x4, waiting for transfers between devices: 5.18 us -> 21.4 us  [swap(): lax.all_to_all(blocks, 'expert', split_axis=0, concat_axis=0, tiled=True)]
    all_to_all x4, starting transfers between devices: 64.8 us -> 51 us  [swap(): lax.all_to_all(blocks, 'expert', split_axis=0, concat_axis=0, tiled=True)]
    unnamed x16 -> x43, local copies, waits for them, and re-layouts: 4.31 us -> 13.5 us
    slice x0 -> x5, local copies, waits for them, and re-layouts: none -> 7.03 us  [the longest x1 2.16 us: turn_down(): backward[half:]]
    pallas_call x2, Pallas kernels: 10.3 us -> 7.33 us  [output_of(): pl.pallas_call(functools.partial(output_kernel, parts), grid=(count // bl...]
    ppermute x17 -> x18, starting transfers between devices: 25 us -> 24 us  [shift_by(): lax.ppermute(value, 'dp', [(i, (i + shift) % splits) for i in range(split...]
  transfers between devices with their start and end apart: 21 -> 22, of which waited for: 13 -> 12; matrix products, arithmetic and copies ran while one was open for 13% -> 18% of each run, Pallas kernels for 11% -> 10%
where the time goes in v4:
time: 244 us; the launch traced here: 243 us
  waiting for transfers between devices  80.7 us (33%)
  starting transfers between devices  75 us (31%)
  Pallas kernels  31.4 us (13%)
  local copies, waits for them, and re-layouts  29.5 us (12%)
  other arithmetic  24.8 us (10%)
    ppermute x18, waiting for transfers between devices, shift_by(): lax.ppermute(value, 'dp', [(i, (i + shift) % splits) for i in range(split...  59.3 us
    all_to_all x4, starting transfers between devices, swap(): lax.all_to_all(blocks, 'expert', split_axis=0, concat_axis=0, tiled=True)  51 us
    ppermute x18, starting transfers between devices, shift_by(): lax.ppermute(value, 'dp', [(i, (i + shift) % splits) for i in range(split...  24 us
    all_to_all x4, waiting for transfers between devices, swap(): lax.all_to_all(blocks, 'expert', split_axis=0, concat_axis=0, tiled=True)  21.4 us
    pallas_call x2, Pallas kernels, hidden_of(): pl.pallas_call(hidden_kernel, grid_spec=pltpu.PrefetchScalarGridSpec(num_...  15.8 us
    unnamed x43, local copies, waits for them, and re-layouts  13.5 us
    another operation x3, other arithmetic, body(): lower_factor = jnp.linalg.cholesky(gram)  12.4 us
    another operation x2, other arithmetic, body(): jax.scipy.linalg.solve_triangular(lower_factor, projected, lower=True)  10.5 us
  transfers between devices with their start and end apart: 22, of which 12 were waited for; matrix products, arithmetic and copies ran while one was open for 18% of the time, Pallas kernels for 10%

profile of v4, /device:TPU:1, one launch (start us, length us, event | category | flops | bytes accessed | tf_op | source)
XLA Modules:
  0.0 243.3 jit_solution(14252385813907414127)
XLA Ops:
  0.6 1.4 copy.13.routes_ref
  2.0 3.2 %dispatch.1 = (bf16[512,1024]{1,0:T(8,128)(2,1)}, bf16[512,1024]{1,0:T(8,128)(2,1)}) custom-call(s32[128,4]{1,0:T(8,128)} %copy.13.routes_ref, bf16[128,1024]{1,0:T(8,128)(2,1)} %tokens_ref.1), custom_call_target="tpu_custom_call" | custom-call | tf_op jit(solution)/shard_map/dispatch/pallas_call | solution.py:47
  5.3 13.2 %all-to-all-start = ((bf16[64,8,1024]{2,1,0:T(8,128)(2,1)}), bf16[64,8,1024]{2,1,0:T(8,128)(2,1)S(1)}, u32[]{:S(2)}, u32[]{:S(2)}) async-start(bf16[64,8,1024]{2,1,0:T(8,128)(2,1)} %bitcast.41), calls=%async_computation | async-start | bytes 2097152 | tf_op jit(solution)/shard_map/all_to_all | solution.py:241
  18.5 1.2 dynamic-slice_bitcast_fusion.3
  19.6 2.7 %dynamic-slice_bitcast_fusion = (bf16[384,1024]{1,0:T(8,128)(2,1)}, bf16[384,1024]{1,0:T(8,128)(2,1)S(1)}, bf16[384,1024]{1,0:T(8,128)(2,1)S(1)}) fusion(bf16[1,384,4096]{2,1,0:T(8,128)(2,1)} %param.12, s32[]{:T(128)S(6)} %select_n.20, s32[]{:T(128)S(6)} %select_n.18, s32[]{:T(128)S(6)} %select_n.19), kind=kLoop, calls=%fused_computation.6 | loop fusion | bytes 4718604 | tf_op jit(solution)/shard_map/dynamic_slice | solution.py:218
  22.4 1.8 fusion.1
  24.2 1.2 collective-permute-start
  25.4 1.5 collective-permute-start.1
  26.9 20.1 %all-to-all-done = bf16[64,8,1024]{2,1,0:T(8,128)(2,1)S(1)} async-done(((bf16[64,8,1024]{2,1,0:T(8,128)(2,1)}), bf16[64,8,1024]{2,1,0:T(8,128)(2,1)S(1)}, u32[]{:S(2)}, u32[]{:S(2)}) %all-to-all-start) | async-done | bytes 1048608 | tf_op jit(solution)/shard_map/all_to_all | solution.py:241
  48.0 6.2 %all-to-all-start.1 = ((bf16[64,8,1024]{2,1,0:T(8,128)(2,1)}), bf16[64,8,1024]{2,1,0:T(8,128)(2,1)S(1)}, u32[]{:S(2)}, u32[]{:S(2)}) async-start(bf16[64,8,1024]{2,1,0:T(8,128)(2,1)} %bitcast.39), calls=%async_computation.1 | async-start | bytes 2097152 | tf_op jit(solution)/shard_map/all_to_all | solution.py:241
  54.2 1.8 collective-permute-done.refs_1_
  56.9 1.8 collective-permute-start.3
  58.7 22.1 %collective-permute-done.2.left_ref = bf16[512,1024]{1,0:T(8,128)(2,1)S(1)} collective-permute-done((bf16[512,1024]{1,0:T(8,128)(2,1)}, bf16[512,1024]{1,0:T(8,128)(2,1)S(1)}, u32[]{:S(2)}, u32[]{:S(2)}) %collective-permute-start.2) | collective-permute-done | bytes 1048608 | tf_op jit(solution)/shard_map/ppermute | solution.py:196
  82.6 2.7 %collective-permute-start.5 = (bf16[256,1024]{1,0:T(8,128)(2,1)}, bf16[256,1024]{1,0:T(8,128)(2,1)}, u32[]{:S(2)}, u32[]{:S(2)}) collective-permute-start(bf16[256,1024]{1,0:T(8,128)(2,1)} %slice.53), channel_id=1, source_target_pairs={{0,192},{64,0},{128,64},{192,128},{1,193},{65,1},{129,65},{193,129... | collective-permute-start | bytes 1572872 | tf_op jit(solution)/shard_map/ppermute | solution.py:196
  85.3 1.8 slice.55
  87.2 1.8 slice.56
  89.0 2.7 %collective-permute-start.10 = (bf16[192,1152]{1,0:T(8,128)(2,1)}, bf16[192,1152]{1,0:T(8,128)(2,1)}, u32[]{:S(2)}, u32[]{:S(2)}) collective-permute-start(bf16[192,1152]{1,0:T(8,128)(2,1)} %slice.56), channel_id=1, source_target_pairs={{0,192},{64,0},{128,64},{192,128},{1,193},{65,1},{129,65},{193,129... | collective-permute-start | bytes 1327112 | tf_op jit(solution)/shard_map/ppermute | solution.py:196
  91.7 1.2 slice.54.refs_5_
  92.9 2.2 slice.57.refs_7_
  96.9 1.2 copy-done.1
  98.1 1.2 copy-done.9
  99.3 1.2 copy-done.11
  101.6 7.9 %hidden.2.refs_0_.refs_2_ = bf16[512,384]{1,0:T(8,128)(2,1)S(1)} custom-call(s32[1]{0:T(128)} %bitcast.me_ref, bf16[512,1024]{1,0:T(8,128)(2,1)S(1)} %copy-done.1, bf16[512,1024]{1,0:T(8,128)(2,1)S(1)} %copy-done.9, bf16[512,1024]{1,0:T(8,128)(2,1)S(1)} %copy-done.11, bf16[256,1024]{1,0:T(8,128)(2,1)S(1)} %copy-done.15, ...), custom_call_target="tpu_custom_call" | custom-call | flops 3221225472 | bytes 10878976 | tf_op jit(solution)/shard_map/hidden/pallas_call | solution.py:105
  109.6 2.0 collective-permute-start.7
  112.2 1.0 constant_dynamic-update-slice_fusion.1
  114.2 1.9 collective-permute-start.12
  116.0 1.1 constant_dynamic-update-slice_fusion.refs_6_
  117.1 4.8 %collective-permute-done.6.refs_1_ = bf16[512,384]{1,0:T(8,128)(2,1)S(1)} collective-permute-done((bf16[512,384]{1,0:T(8,128)(2,1)S(1)}, bf16[512,384]{1,0:T(8,128)(2,1)S(1)}, u32[]{:S(2)}, u32[]{:S(2)}) %collective-permute-start.6) | collective-permute-done | bytes 393248 | tf_op jit(solution)/shard_map/ppermute | solution.py:196
  122.5 5.1 %collective-permute-done.8.refs_3_ = bf16[512,384]{1,0:T(8,128)(2,1)S(1)} collective-permute-done((bf16[512,384]{1,0:T(8,128)(2,1)S(1)}, bf16[512,384]{1,0:T(8,128)(2,1)S(1)}, u32[]{:S(2)}, u32[]{:S(2)}) %collective-permute-start.8) | collective-permute-done | bytes 393248 | tf_op jit(solution)/shard_map/ppermute | solution.py:196
  127.6 3.7 %output.2 = (bf16[512,1024]{1,0:T(8,128)(2,1)}, f32[512,128]{1,0:T(8,128)S(1)}) custom-call(bf16[512,384]{1,0:T(8,128)(2,1)S(1)} %hidden.2.refs_0_.refs_2_, bf16[512,384]{1,0:T(8,128)(2,1)S(1)} %collective-permute-done.6.refs_1_, bf16[512,384]{1,0:T(8,128)(2,1)S(1)} %collective-permute-done.7.refs_2_, bf16[512,384]{1,0:T(8,128)(2,1)S(1)} %collective-permute-done.8.refs_3_, ...), custom_call_target="tpu_custom_call" | custom-call | flops 1811939328 | bytes 7471104 | tf_op jit(solution)/shard_map/output/pallas_call | solution.py:137
  131.2 19.7 %all-to-all-start.2 = ((bf16[64,8,1024]{2,1,0:T(8,128)(2,1)}), bf16[64,8,1024]{2,1,0:T(8,128)(2,1)}, u32[]{:S(2)}, u32[]{:S(2)}) async-start(bf16[64,8,1024]{2,1,0:T(8,128)(2,1)} %bitcast.42), calls=%async_computation.2 | async-start | bytes 2097152 | tf_op jit(solution)/shard_map/all_to_all | solution.py:241
  151.0 1.1 slice.58
  152.1 1.1 slice.59
  153.2 3.0 %collective-permute-start.14 = (bf16[256,1024]{1,0:T(8,128)(2,1)S(1)}, bf16[256,1024]{1,0:T(8,128)(2,1)S(1)}, u32[]{:S(2)}, u32[]{:S(2)}) collective-permute-start(bf16[256,1024]{1,0:T(8,128)(2,1)S(1)} %slice.59), channel_id=1, source_target_pairs={{0,192},{64,0},{128,64},{192,128},{1,193},{65,1},{129,65},{193,129... | collective-permute-start | bytes 1572872 | tf_op jit(solution)/shard_map/ppermute | solution.py:196
  156.2 8.3 %collective-permute-done.13.top_ref = bf16[256,1024]{1,0:T(8,128)(2,1)S(1)} collective-permute-done((bf16[256,1024]{1,0:T(8,128)(2,1)S(1)}, bf16[256,1024]{1,0:T(8,128)(2,1)S(1)}, u32[]{:S(2)}, u32[]{:S(2)}) %collective-permute-start.13) | collective-permute-done | bytes 524320 | tf_op jit(solution)/shard_map/ppermute | solution.py:196
  164.8 7.9 %hidden.3.refs_0_.refs_3_ = bf16[512,384]{1,0:T(8,128)(2,1)S(1)} custom-call(s32[1]{0:T(128)} %bitcast.me_ref, bf16[512,1024]{1,0:T(8,128)(2,1)S(1)} %bitcast.38, bf16[512,1024]{1,0:T(8,128)(2,1)} %collective-permute-done.11.left_ref, bf16[512,1024]{1,0:T(8,128)(2,1)} %collective-permute-done.12.right_ref, ...), custom_call_target="tpu_custom_call" | custom-call | flops 3221225472 | bytes 10878976 | tf_op jit(solution)/shard_map/hidden/pallas_call | solution.py:105
  173.3 4.2 %collective-permute-start.16 = (bf16[512,384]{1,0:T(8,128)(2,1)S(1)}, bf16[512,384]{1,0:T(8,128)(2,1)S(1)}, u32[]{:S(2)}, u32[]{:S(2)}) collective-permute-start(bf16[512,384]{1,0:T(8,128)(2,1)S(1)} %hidden.3.refs_0_.refs_3_), channel_id=1, source_target_pairs={{0,128},{64,192},{128,0},{192,64},{1,129},{65,193},{129,1},{193,65... | collective-permute-start | bytes 1179656 | tf_op jit(solution)/shard_map/ppermute | solution.py:196
  177.5 4.8 %collective-permute-done.15.refs_1_ = bf16[512,384]{1,0:T(8,128)(2,1)S(1)} collective-permute-done((bf16[512,384]{1,0:T(8,128)(2,1)S(1)}, bf16[512,384]{1,0:T(8,128)(2,1)S(1)}, u32[]{:S(2)}, u32[]{:S(2)}) %collective-permute-start.15) | collective-permute-done | bytes 393248 | tf_op jit(solution)/shard_map/ppermute | solution.py:196
  182.4 9.3 %collective-permute-done.16.refs_2_ = bf16[512,384]{1,0:T(8,128)(2,1)S(1)} collective-permute-done((bf16[512,384]{1,0:T(8,128)(2,1)S(1)}, bf16[512,384]{1,0:T(8,128)(2,1)S(1)}, u32[]{:S(2)}, u32[]{:S(2)}) %collective-permute-start.16) | collective-permute-done | bytes 393248 | tf_op jit(solution)/shard_map/ppermute | solution.py:196
  191.7 2.2 collective-permute-done.17.refs_3_
  193.9 3.7 %output.3 = (bf16[512,1024]{1,0:T(8,128)(2,1)}, f32[512,128]{1,0:T(8,128)S(1)}) custom-call(bf16[512,384]{1,0:T(8,128)(2,1)S(1)} %hidden.3.refs_0_.refs_3_, bf16[512,384]{1,0:T(8,128)(2,1)S(1)} %collective-permute-done.15.refs_1_, bf16[512,384]{1,0:T(8,128)(2,1)S(1)} %collective-permute-done.16.refs_2_, ...), custom_call_target="tpu_custom_call" | custom-call | flops 1811939328 | bytes 7471104 | tf_op jit(solution)/shard_map/output/pallas_call | solution.py:137
  198.3 11.9 %all-to-all-start.3 = ((bf16[64,8,1024]{2,1,0:T(8,128)(2,1)}), bf16[64,8,1024]{2,1,0:T(8,128)(2,1)S(1)}, u32[]{:S(2)}, u32[]{:S(2)}) async-start(bf16[64,8,1024]{2,1,0:T(8,128)(2,1)} %bitcast.43), calls=%async_computation.3 | async-start | bytes 2097152 | tf_op jit(solution)/shard_map/all_to_all | solution.py:241
  212.0 1.5 moments.1
  213.6 11.7 %cholesky.16 = f32[128,128]{1,0:T(8,128)S(1)} custom-call(f32[128,128]{1,0:T(8,128)S(1)} %fusion.4), custom_call_target="Cholesky" | custom-call | tf_op jit(solution)/shard_map/jit(cholesky)/cholesky | solution.py:269
  226.7 9.8 %custom-call.7 = f32[1,128,128]{1,2,0:T(8,128)S(1)} custom-call(f32[1,128,128]{2,1,0:T(8,128)S(1)} %fusion.2), custom_call_target="InvertDiagBlocksLowerTriangular" | custom-call | tf_op jit(solution)/shard_map/jit(_solve_triangular)/triangular_solve | solution.py:270
  236.5 1.1 convolution_bitcast_fusion
  237.5 1.3 all-to-all-done.3
  239.8 3.5 %combine.1 = bf16[128,1024]{1,0:T(8,128)(2,1)} custom-call(s32[128,4]{1,0:T(8,128)} %copy.13.routes_ref, f32[128,4]{1,0:T(8,128)} %copy.14.weights_ref, bf16[512,1024]{1,0:T(8,128)(2,1)} %bitcast.13.refs_0_, bf16[512,1024]{1,0:T(8,128)(2,1)} %bitcast.40), custom_call_target="tpu_custom_call" | custom-call | tf_op jit(solution)/shard_map/combine/pallas_call | solution.py:75
  (71 shorter events, 14.7 us)
Async XLA Ops:
  5.3 41.7 %all-to-all-start = ((bf16[64,8,1024]{2,1,0:T(8,128)(2,1)}), bf16[64,8,1024]{2,1,0:T(8,128)(2,1)S(1)}, u32[]{:S(2)}, u32[]{:S(2)}) async-start(bf16[64,8,1024]{2,1,0:T(8,128)(2,1)} %bitcast.41), calls=%async_computation | async-start | bytes 2097152 | tf_op jit(solution)/shard_map/all_to_all | solution.py:241
  19.6 2.8 %copy-start.18 = (bf16[384,128]{1,0:T(8,128)(2,1)S(1)}, bf16[384,128]{1,0:T(8,128)(2,1)}, u32[]{:S(2)}) copy-start(bf16[384,128]{1,0:T(8,128)(2,1)} %param.13) | copy-start | bytes 294916
  24.2 31.8 %collective-permute-start = (bf16[576,1152]{1,0:T(8,128)(2,1)}, bf16[576,1152]{1,0:T(8,128)(2,1)}, u32[]{:S(2)}, u32[]{:S(2)}) collective-permute-start(bf16[576,1152]{1,0:T(8,128)(2,1)} %get-tuple-element.24), channel_id=1, source_target_pairs={{0,64},{64,128},{128,192},{192,0},{1,65},{65,129},{129,193},{193,1... | collective-permute-start | bytes 3981320 | tf_op jit(solution)/shard_map/ppermute | solution.py:196
  25.4 30.6 %collective-permute-start.1 = (bf16[576,1152]{1,0:T(8,128)(2,1)}, bf16[576,1152]{1,0:T(8,128)(2,1)}, u32[]{:S(2)}, u32[]{:S(2)}) collective-permute-start(bf16[576,1152]{1,0:T(8,128)(2,1)} %get-tuple-element.23), channel_id=1, source_target_pairs={{0,192},{64,0},{128,64},{192,128},{1,193},{65,1},{129,65},{193,129... | collective-permute-start | bytes 3981320 | tf_op jit(solution)/shard_map/ppermute | solution.py:196
  47.0 1.0 copy-start
  48.0 47.1 %all-to-all-start.1 = ((bf16[64,8,1024]{2,1,0:T(8,128)(2,1)}), bf16[64,8,1024]{2,1,0:T(8,128)(2,1)S(1)}, u32[]{:S(2)}, u32[]{:S(2)}) async-start(bf16[64,8,1024]{2,1,0:T(8,128)(2,1)} %bitcast.39), calls=%async_computation.1 | async-start | bytes 2097152 | tf_op jit(solution)/shard_map/all_to_all | solution.py:241
  56.0 31.1 %copy-start.17 = (bf16[384,1024]{1,0:T(8,128)(2,1)S(1)}, bf16[384,1024]{1,0:T(8,128)(2,1)}, u32[]{:S(2)}) copy-start(bf16[384,1024]{1,0:T(8,128)(2,1)} %get-tuple-element.18) | copy-start | bytes 2359300
  56.0 24.8 %collective-permute-start.2 = (bf16[512,1024]{1,0:T(8,128)(2,1)}, bf16[512,1024]{1,0:T(8,128)(2,1)S(1)}, u32[]{:S(2)}, u32[]{:S(2)}) collective-permute-start(bf16[512,1024]{1,0:T(8,128)(2,1)} %after.3.refs_0_), channel_id=1, source_target_pairs={{0,64},{64,128},{128,192},{192,0},{1,65},{65,129},{129,193},{193,1... | collective-permute-start | bytes 3145736 | tf_op jit(solution)/shard_map/ppermute | solution.py:196
  56.9 24.8 %collective-permute-start.3 = (bf16[512,1024]{1,0:T(8,128)(2,1)}, bf16[512,1024]{1,0:T(8,128)(2,1)S(1)}, u32[]{:S(2)}, u32[]{:S(2)}) collective-permute-start(bf16[512,1024]{1,0:T(8,128)(2,1)} %after.3.refs_0_), channel_id=1, source_target_pairs={{0,192},{64,0},{128,64},{192,128},{1,193},{65,1},{129,65},{193,129... | collective-permute-start | bytes 3145736 | tf_op jit(solution)/shard_map/ppermute | solution.py:196
  80.8 6.3 %copy-start.8 = (bf16[512,1024]{1,0:T(8,128)(2,1)}, bf16[512,1024]{1,0:T(8,128)(2,1)S(1)}, u32[]{:S(2)}) copy-start(bf16[512,1024]{1,0:T(8,128)(2,1)S(1)} %collective-permute-done.2.left_ref) | copy-start | bytes 3145732
  81.7 14.4 %collective-permute-start.4 = (bf16[256,1024]{1,0:T(8,128)(2,1)}, bf16[256,1024]{1,0:T(8,128)(2,1)S(1)}, u32[]{:S(2)}, u32[]{:S(2)}) collective-permute-start(bf16[256,1024]{1,0:T(8,128)(2,1)} %slice.52), channel_id=1, source_target_pairs={{0,64},{64,128},{128,192},{192,0},{1,65},{65,129},{129,193},{193,1... | collective-permute-start | bytes 1572872 | tf_op jit(solution)/shard_map/ppermute | solution.py:196
  81.7 5.4 %copy-start.10 = (bf16[512,1024]{1,0:T(8,128)(2,1)}, bf16[512,1024]{1,0:T(8,128)(2,1)S(1)}, u32[]{:S(2)}) copy-start(bf16[512,1024]{1,0:T(8,128)(2,1)S(1)} %collective-permute-done.3.right_ref) | copy-start | bytes 3145732
  82.6 14.3 %collective-permute-start.5 = (bf16[256,1024]{1,0:T(8,128)(2,1)}, bf16[256,1024]{1,0:T(8,128)(2,1)}, u32[]{:S(2)}, u32[]{:S(2)}) collective-permute-start(bf16[256,1024]{1,0:T(8,128)(2,1)} %slice.53), channel_id=1, source_target_pairs={{0,192},{64,0},{128,64},{192,128},{1,193},{65,1},{129,65},{193,129... | collective-permute-start | bytes 1572872 | tf_op jit(solution)/shard_map/ppermute | solution.py:196
  87.1 25.2 %collective-permute-start.9 = (bf16[192,1152]{1,0:T(8,128)(2,1)}, bf16[192,1152]{1,0:T(8,128)(2,1)}, u32[]{:S(2)}, u32[]{:S(2)}) collective-permute-start(bf16[192,1152]{1,0:T(8,128)(2,1)} %slice.55), channel_id=1, source_target_pairs={{0,64},{64,128},{128,192},{192,0},{1,65},{65,129},{129,193},{193,1... | collective-permute-start | bytes 1327112 | tf_op jit(solution)/shard_map/ppermute | solution.py:196
  89.0 25.2 %collective-permute-start.10 = (bf16[192,1152]{1,0:T(8,128)(2,1)}, bf16[192,1152]{1,0:T(8,128)(2,1)}, u32[]{:S(2)}, u32[]{:S(2)}) collective-permute-start(bf16[192,1152]{1,0:T(8,128)(2,1)} %slice.56), channel_id=1, source_target_pairs={{0,192},{64,0},{128,64},{192,128},{1,193},{65,1},{129,65},{193,129... | collective-permute-start | bytes 1327112 | tf_op jit(solution)/shard_map/ppermute | solution.py:196
  95.1 1.0 copy-start.2
  96.1 0.8 copy-start.14
  96.9 1.2 copy-start.1
  98.1 1.2 copy-start.9
  99.3 1.2 copy-start.11
  100.5 1.0 copy-start.15
  101.6 11.7 %copy-start.3 = (bf16[64,8,1024]{2,1,0:T(8,128)(2,1)S(1)}, bf16[64,8,1024]{2,1,0:T(8,128)(2,1)}, u32[]{:S(2)}) copy-start(bf16[64,8,1024]{2,1,0:T(8,128)(2,1)} %copy-done.2) | copy-start | bytes 3145732
  101.6 26.0 %copy-start.4 = (bf16[384,1152]{1,0:T(8,128)(2,1)S(1)}, bf16[384,1152]{1,0:T(8,128)(2,1)}, u32[]{:S(2)}) copy-start(bf16[384,1152]{1,0:T(8,128)(2,1)} %slice.57.refs_7_) | copy-start | bytes 2654212
  109.5 12.5 %collective-permute-start.6 = (bf16[512,384]{1,0:T(8,128)(2,1)S(1)}, bf16[512,384]{1,0:T(8,128)(2,1)S(1)}, u32[]{:S(2)}, u32[]{:S(2)}) collective-permute-start(bf16[512,384]{1,0:T(8,128)(2,1)S(1)} %hidden.2.refs_0_.refs_2_), channel_id=1, source_target_pairs={{0,64},{64,128},{128,192},{192,0},{1,65},{65,129},{129,193},{193,1... | collective-permute-start | bytes 1179656 | tf_op jit(solution)/shard_map/ppermute | solution.py:196
  109.6 12.9 %collective-permute-start.7 = (bf16[512,384]{1,0:T(8,128)(2,1)S(1)}, bf16[512,384]{1,0:T(8,128)(2,1)S(1)}, u32[]{:S(2)}, u32[]{:S(2)}) collective-permute-start(bf16[512,384]{1,0:T(8,128)(2,1)S(1)} %hidden.2.refs_0_.refs_2_), channel_id=1, source_target_pairs={{0,128},{64,192},{128,0},{192,64},{1,129},{65,193},{129,1},{193,65... | collective-permute-start | bytes 1179656 | tf_op jit(solution)/shard_map/ppermute | solution.py:196
  111.6 16.0 %collective-permute-start.8 = (bf16[512,384]{1,0:T(8,128)(2,1)S(1)}, bf16[512,384]{1,0:T(8,128)(2,1)S(1)}, u32[]{:S(2)}, u32[]{:S(2)}) collective-permute-start(bf16[512,384]{1,0:T(8,128)(2,1)S(1)} %hidden.2.refs_0_.refs_2_), channel_id=1, source_target_pairs={{0,192},{64,0},{128,64},{192,128},{1,193},{65,1},{129,65},{193,129... | collective-permute-start | bytes 1179656 | tf_op jit(solution)/shard_map/ppermute | solution.py:196
  113.3 37.7 %collective-permute-start.11 = (bf16[512,1024]{1,0:T(8,128)(2,1)S(1)}, bf16[512,1024]{1,0:T(8,128)(2,1)}, u32[]{:S(2)}, u32[]{:S(2)}) collective-permute-start(bf16[512,1024]{1,0:T(8,128)(2,1)S(1)} %bitcast.36), channel_id=1, source_target_pairs={{0,64},{64,128},{128,192},{192,0},{1,65},{65,129},{129,193},{193,1... | collective-permute-start | bytes 3145736 | tf_op jit(solution)/shard_map/ppermute | solution.py:196
  114.2 38.0 %collective-permute-start.12 = (bf16[512,1024]{1,0:T(8,128)(2,1)S(1)}, bf16[512,1024]{1,0:T(8,128)(2,1)}, u32[]{:S(2)}, u32[]{:S(2)}) collective-permute-start(bf16[512,1024]{1,0:T(8,128)(2,1)S(1)} %bitcast.37), channel_id=1, source_target_pairs={{0,192},{64,0},{128,64},{192,128},{1,193},{65,1},{129,65},{193,129... | collective-permute-start | bytes 3145736 | tf_op jit(solution)/shard_map/ppermute | solution.py:196
  117.1 14.1 %copy-start.12 = (bf16[384,1152]{1,0:T(8,128)(2,1)}, bf16[384,1152]{1,0:T(8,128)(2,1)S(1)}, u32[]{:S(2)}) copy-start(bf16[384,1152]{1,0:T(8,128)(2,1)S(1)} %constant_dynamic-update-slice_fusion.refs_6_) | copy-start | bytes 2654212
  131.2 67.0 %all-to-all-start.2 = ((bf16[64,8,1024]{2,1,0:T(8,128)(2,1)}), bf16[64,8,1024]{2,1,0:T(8,128)(2,1)}, u32[]{:S(2)}, u32[]{:S(2)}) async-start(bf16[64,8,1024]{2,1,0:T(8,128)(2,1)} %bitcast.42), calls=%async_computation.2 | async-start | bytes 2097152 | tf_op jit(solution)/shard_map/all_to_all | solution.py:241
  152.0 12.5 %collective-permute-start.13 = (bf16[256,1024]{1,0:T(8,128)(2,1)S(1)}, bf16[256,1024]{1,0:T(8,128)(2,1)S(1)}, u32[]{:S(2)}, u32[]{:S(2)}) collective-permute-start(bf16[256,1024]{1,0:T(8,128)(2,1)S(1)} %slice.58), channel_id=1, source_target_pairs={{0,64},{64,128},{128,192},{192,0},{1,65},{65,129},{129,193},{193,1... | collective-permute-start | bytes 1572872 | tf_op jit(solution)/shard_map/ppermute | solution.py:196
  153.2 40.6 %copy-start.5 = (bf16[384,1152]{1,0:T(8,128)(2,1)S(1)}, bf16[384,1152]{1,0:T(8,128)(2,1)}, u32[]{:S(2)}) copy-start(bf16[384,1152]{1,0:T(8,128)(2,1)} %slice.57.refs_7_) | copy-start | bytes 2654212
  153.2 40.6 %copy-start.13 = (bf16[384,1152]{1,0:T(8,128)(2,1)S(1)}, bf16[384,1152]{1,0:T(8,128)(2,1)}, u32[]{:S(2)}) copy-start(bf16[384,1152]{1,0:T(8,128)(2,1)} %copy-done.12) | copy-start | bytes 2654212
  153.2 11.6 %collective-permute-start.14 = (bf16[256,1024]{1,0:T(8,128)(2,1)S(1)}, bf16[256,1024]{1,0:T(8,128)(2,1)S(1)}, u32[]{:S(2)}, u32[]{:S(2)}) collective-permute-start(bf16[256,1024]{1,0:T(8,128)(2,1)S(1)} %slice.59), channel_id=1, source_target_pairs={{0,192},{64,0},{128,64},{192,128},{1,193},{65,1},{129,65},{193,129... | collective-permute-start | bytes 1572872 | tf_op jit(solution)/shard_map/ppermute | solution.py:196
  172.7 37.5 %copy-start.19 = (f32[128,4]{0,1:T(4,128)S(1)}, f32[128,4]{0,1:T(4,128)}, u32[]{:S(2)}) copy-start(f32[128,4]{0,1:T(4,128)} %param.9) | copy-start | bytes 6148
  172.8 9.6 %collective-permute-start.15 = (bf16[512,384]{1,0:T(8,128)(2,1)S(1)}, bf16[512,384]{1,0:T(8,128)(2,1)S(1)}, u32[]{:S(2)}, u32[]{:S(2)}) collective-permute-start(bf16[512,384]{1,0:T(8,128)(2,1)S(1)} %hidden.3.refs_0_.refs_3_), channel_id=1, source_target_pairs={{0,64},{64,128},{128,192},{192,0},{1,65},{65,129},{129,193},{193,1... | collective-permute-start | bytes 1179656 | tf_op jit(solution)/shard_map/ppermute | solution.py:196
  173.3 18.3 %collective-permute-start.16 = (bf16[512,384]{1,0:T(8,128)(2,1)S(1)}, bf16[512,384]{1,0:T(8,128)(2,1)S(1)}, u32[]{:S(2)}, u32[]{:S(2)}) collective-permute-start(bf16[512,384]{1,0:T(8,128)(2,1)S(1)} %hidden.3.refs_0_.refs_3_), channel_id=1, source_target_pairs={{0,128},{64,192},{128,0},{192,64},{1,129},{65,193},{129,1},{193,65... | collective-permute-start | bytes 1179656 | tf_op jit(solution)/shard_map/ppermute | solution.py:196
  177.5 16.3 %collective-permute-start.17 = (bf16[512,384]{1,0:T(8,128)(2,1)S(1)}, bf16[512,384]{1,0:T(8,128)(2,1)S(1)}, u32[]{:S(2)}, u32[]{:S(2)}) collective-permute-start(bf16[512,384]{1,0:T(8,128)(2,1)S(1)} %hidden.3.refs_0_.refs_3_), channel_id=1, source_target_pairs={{0,192},{64,0},{128,64},{192,128},{1,193},{65,1},{129,65},{193,129... | collective-permute-start | bytes 1179656 | tf_op jit(solution)/shard_map/ppermute | solution.py:196
  197.5 0.7 copy-start.6
  198.3 40.5 %all-to-all-start.3 = ((bf16[64,8,1024]{2,1,0:T(8,128)(2,1)}), bf16[64,8,1024]{2,1,0:T(8,128)(2,1)S(1)}, u32[]{:S(2)}, u32[]{:S(2)}) async-start(bf16[64,8,1024]{2,1,0:T(8,128)(2,1)} %bitcast.43), calls=%async_computation.3 | async-start | bytes 2097152 | tf_op jit(solution)/shard_map/all_to_all | solution.py:241
  211.0 1.0 copy-start.7
  238.8 1.0 copy-start.16
